TPU v7x, 512 devices: a whole 4x8x8 slice. The times are simulated.
512 devices in a mesh: row: 128 (over z, x_hi, y), col: 4 (over x_lo, core).
Axes of the slice: x: 4 (x_hi: 2, x_lo: 2; x = x_hi * 2 + x_lo), y: 8, z: 8, core: 2. Of those that a mesh axis runs over, the one named last changes fastest.
Arguments:
- features: bfloat16 [131072, 256], P(('row', 'col')), may hold values from -6 to 6
- weight: bfloat16 [256, 256], replicated, may hold values from -0.375 to 0.375
- bias: float32 [256], replicated, may hold values from -3 to 3
- block_values: bfloat16 [128, 4, 32, 128, 128], P('row', 'col'), may hold values from -0.1875 to 0.1875
- block_target: int32 [128, 4, 32], P('row', 'col'), may hold values from 0 to 9
- block_source: int32 [128, 4, 32], P('row', 'col'), may hold values from 0 to 7
- block_count: int32 [128, 4], P('row', 'col'), may hold values from 4 to 32, as said below
- cotangent: bfloat16 [131072, 256], P(('row', 'col')), may hold values from -6 to 6
Outputs:
- output: bfloat16 [131072, 256], P(('row', 'col'))
- grad_inputs: bfloat16 [131072, 256], P(('row', 'col'))
- grad_weight: float32 [256, 256], replicated
- grad_bias: float32 [256], replicated
Inputs may be any that keep to these rules, and one draw needn't show every extreme that they name: `block_count`: slots at or after a device's count hold no adjacency block; some device uses all 32 slots.
All inputs are finite; a program needn't handle non-finite values.
Results may differ from a plain program's by a relative error of at most 0.006.
Values may be sent and summed in bfloat16 or wider, within the bound.
A program may use at most 64 MiB of HBM per device.

v0:
```python
import math

import jax
import jax.numpy as jnp
from jax import lax
from jax.sharding import PartitionSpec as P

BLK = 128
HALF = 2
VB = 2


def shifted(block, axis, distance):
    devices = range(lax.axis_size(axis))
    route = [((i - distance) % len(devices), i) for i in devices]
    return lax.ppermute(block, axis, route)


def silu_slope(argument):
    sigmoid_value = jax.nn.sigmoid(argument)
    return sigmoid_value * (1.0 + argument * (1.0 - sigmoid_value))


def shards(
    features, weight, bias, block_values, block_target, block_source, block_count, cotangent
):
    span_count = 2 * HALF + 1
    slot_total = block_values.shape[2]
    group_size = min(slot_total, 32)
    group_total = slot_total // group_size
    columns = lax.axis_size("col")
    rows_own = features.shape[0]
    feature_width = features.shape[1]
    source_total = columns * VB
    dest_total = span_count * VB
    values_own = block_values[0, 0]
    target_own = block_target[0, 0]
    source_own = block_source[0, 0]
    live_count = block_count[0, 0]
    hidden = jnp.dot(features, weight, preferred_element_type=jnp.float32).astype(jnp.bfloat16)
    row_sources = lax.all_gather(hidden, "col", axis=0, tiled=True).reshape(
        source_total, BLK, feature_width
    )

    def slot_slice(slot_start):
        live_part = (slot_start + jnp.arange(group_size, dtype=jnp.int32) < live_count).astype(
            jnp.float32
        )
        return (values_own, target_own, source_own, live_part)

    def forward_group(group_index, totals):
        slot_start = group_index * group_size

        def forward_add_group(current):
            block_part, target_part, source_part, live_part = slot_slice(slot_start)
            picked = jnp.take(row_sources, source_part, axis=0)
            products = jnp.einsum(
                "sij,sjf->sif", block_part, picked, preferred_element_type=jnp.float32
            )
            selector = (
                target_part[None, :] == jnp.arange(dest_total, dtype=jnp.int32)[:, None]
            ).astype(jnp.float32) * live_part[None, :]
            return current + jnp.einsum(
                "ds,sif->dif", selector, products, precision=lax.Precision.HIGHEST
            )

        return lax.cond(slot_start < live_count, forward_add_group, lambda current: current, totals)

    partial_value = lax.fori_loop(
        0, group_total, forward_group, jnp.zeros((dest_total, BLK, feature_width), jnp.float32)
    )
    partial_value = partial_value.reshape(span_count, VB, BLK, feature_width)
    aggregate = partial_value[HALF]
    for distance in range(1, HALF + 1):
        aggregate = aggregate + shifted(partial_value[HALF + distance], "row", distance)
        aggregate = aggregate + shifted(partial_value[HALF - distance], "row", -distance)
    pre_value = aggregate.reshape(rows_own, feature_width) + bias[None, :]
    output = jax.nn.silu(pre_value).astype(jnp.bfloat16)
    grad_pre_exact = cotangent.astype(jnp.float32) * silu_slope(pre_value)
    grad_pre = grad_pre_exact.astype(jnp.bfloat16)
    local_grad = grad_pre.reshape(VB, BLK, feature_width)
    from_above = []
    behind = []
    for distance in range(1, HALF + 1):
        from_above.append(shifted(local_grad, "row", -distance))
        behind.append(shifted(local_grad, "row", distance))
    fetched = jnp.concatenate(behind[::-1] + [local_grad] + from_above, axis=0)

    def backward_group(group_index, totals):
        slot_start = group_index * group_size

        def backward_add_group(current):
            block_part, target_part, source_part, live_part = slot_slice(slot_start)
            picked = jnp.take(fetched, target_part, axis=0)
            products = jnp.einsum(
                "sji,sjf->sif", block_part, picked, preferred_element_type=jnp.float32
            )
            selector = (
                source_part[None, :] == jnp.arange(source_total, dtype=jnp.int32)[:, None]
            ).astype(jnp.float32) * live_part[None, :]
            return current + jnp.einsum(
                "bs,sif->bif", selector, products, precision=lax.Precision.HIGHEST
            )

        return lax.cond(
            slot_start < live_count, backward_add_group, lambda current: current, totals
        )

    source_terms = lax.fori_loop(
        0, group_total, backward_group, jnp.zeros((source_total, BLK, feature_width), jnp.float32)
    )
    source_terms = source_terms.reshape(source_total * BLK, feature_width)
    grad_source = lax.psum_scatter(source_terms, "col", scatter_dimension=0, tiled=True).astype(
        jnp.bfloat16
    )
    grad_inputs = lax.dot_general(
        grad_source, weight, (((1,), (1,)), ((), ())), preferred_element_type=jnp.float32
    ).astype(jnp.bfloat16)
    weight_term = lax.dot_general(
        features, grad_source, (((0,), (0,)), ((), ())), preferred_element_type=jnp.float32
    )
    bias_term = jnp.sum(grad_pre_exact, axis=0)
    weight_total, bias_total = lax.psum((weight_term, bias_term), ("row", "col"))
    normalizer = 1.0 / math.sqrt(rows_own * lax.axis_size("row") * columns)
    return (output, grad_inputs, weight_total * normalizer, bias_total * normalizer)


def solution(mesh):
    return jax.shard_map(
        shards,
        mesh=mesh,
        in_specs=(
            P(("row", "col"), None),
            P(),
            P(),
            P("row", "col", None, None, None),
            P("row", "col", None),
            P("row", "col", None),
            P("row", "col"),
            P(("row", "col"), None),
        ),
        out_specs=(P(("row", "col"), None), P(("row", "col"), None), P(), P()),
        check_vma=False,
    )
```

profile of v0, /device:TPU:1, one launch (start us, length us, event | category | flops | bytes accessed | tf_op | source)
XLA Modules:
  0.0 488.4 jit_solution(17895066004449689747)
XLA Ops:
  7.2 0.8 copy-done
  8.1 1.1 convolution_convert_fusion.1
  9.2 13.2 %all_gather.3 = bf16[1024,256]{1,0:T(8,128)(2,1)S(1)} all-gather(bf16[256,256]{1,0:T(8,128)(2,1)S(1)} %convolution_convert_fusion.1), channel_id=1, replica_groups=mesh['row'=128,'col'=4] {'col'}, dimensions={0}, use_global_device_ids=true | all-gather | bytes 655360 | tf_op jit(solution)/shard_map/all_gather | solution.py:41
  23.3 16.9 %conditional.2 = (f32[10,128,256]{2,0,1:T(8,128)S(1)}) conditional(s32[]{:T(128)} %convert_element_type.40, f32[10,128,256]{2,0,1:T(8,128)S(1)} %broadcast_in_dim.33, (s32[1,1,32]{2,1,0:T(1,128)S(1)}, s32[]{:T(128)}, s32[1,1,32]{2,1,0:T(1,128)S(1)}, bf16[1024,256]{1,0:T(8,128)(2,1)S(1)}, bf16[32,128,128]{2,1,0:T(8,128)(2,1)}, ...), branch_computations={%region_0.1_spmd, %region_1.2_spmd} | conditional | flops 395642848 | bytes 26743884 | solution.py:67
  24.0 2.0 gather_fusion
  26.1 4.6 fusion.2
  30.7 5.5 %copy.17 = f32[32,256,128]{1,0,2:T(8,128)} copy(f32[32,256,128]{2,1,0:T(8,128)} %fusion.2) | data formatting | bytes 8388608 | tf_op jit(solution)/shard_map/while/body/eval_jaxpr/cond/branch_1_fun/sij,sjf->sif/dot_general | solution.py:57
  36.2 4.0 fusion.5
  40.6 1.9 collective-permute-start
  42.5 11.0 %collective-permute-start.1 = (f32[2,128,256]{2,0,1:T(2,128)S(1)}, f32[2,128,256]{2,0,1:T(2,128)S(1)}, u32[]{:S(2)}, u32[]{:S(2)}) collective-permute-start(f32[2,128,256]{2,0,1:T(2,128)S(1)} %get-tuple-element.120), channel_id=1, source_target_pairs={{4,0},{8,4},{12,8},{16,12},{20,16},{24,20},{28,24},{32,28},{36,32}... | collective-permute-start | bytes 786440 | tf_op jit(solution)/shard_map/ppermute | solution.py:16
  53.6 1.9 collective-permute-start.2
  55.5 10.0 %collective-permute-start.3 = (f32[2,128,256]{2,0,1:T(2,128)S(1)}, f32[2,128,256]{2,0,1:T(2,128)S(1)}, u32[]{:S(2)}, u32[]{:S(2)}) collective-permute-start(f32[2,128,256]{2,0,1:T(2,128)S(1)} %get-tuple-element.118), channel_id=1, source_target_pairs={{8,0},{12,4},{16,8},{20,12},{24,16},{28,20},{32,24},{36,28},{40,32... | collective-permute-start | bytes 786440 | tf_op jit(solution)/shard_map/ppermute | solution.py:16
  65.5 7.6 %collective-permute-done.2 = f32[2,128,256]{2,0,1:T(2,128)S(1)} collective-permute-done((f32[2,128,256]{2,0,1:T(2,128)S(1)}, f32[2,128,256]{2,0,1:T(2,128)S(1)}, u32[]{:S(2)}, u32[]{:S(2)}) %collective-permute-start.2) | collective-permute-done | bytes 262176 | tf_op jit(solution)/shard_map/ppermute | solution.py:16
  73.1 3.6 collective-permute-done.3
  77.1 0.8 fusion.39
  77.9 1.9 collective-permute-start.4
  79.8 1.9 collective-permute-start.5
  81.7 9.1 %collective-permute-start.6 = (bf16[2,128,256]{2,1,0:T(8,128)(2,1)S(1)}, bf16[2,128,256]{2,1,0:T(8,128)(2,1)S(1)}, u32[]{:S(2)}, u32[]{:S(2)}) collective-permute-start(bf16[2,128,256]{2,1,0:T(8,128)(2,1)S(1)} %bitcast.57), channel_id=1, source_target_pairs={{4,0},{8,4},{12,8},{16,12},{20,16},{24,20},{28,24},{32,28},{36,32}... | collective-permute-start | bytes 393224 | tf_op jit(solution)/shard_map/ppermute | solution.py:16
  90.8 5.0 %collective-permute-start.7 = (bf16[2,128,256]{2,1,0:T(8,128)(2,1)S(1)}, bf16[2,128,256]{2,1,0:T(8,128)(2,1)S(1)}, u32[]{:S(2)}, u32[]{:S(2)}) collective-permute-start(bf16[2,128,256]{2,1,0:T(8,128)(2,1)S(1)} %bitcast.58), channel_id=1, source_target_pairs={{8,0},{12,4},{16,8},{20,12},{24,16},{28,20},{32,24},{36,28},{40,32... | collective-permute-start | bytes 393224 | tf_op jit(solution)/shard_map/ppermute | solution.py:16
  98.5 0.7 constant_dynamic-update-slice_fusion
  99.3 15.9 %conditional.3 = (f32[8,128,256]{2,0,1:T(8,128)S(1)}) conditional(s32[]{:T(128)} %convert_element_type.40, f32[8,128,256]{2,0,1:T(8,128)S(1)} %broadcast_in_dim.34, (s32[1,1,32]{2,1,0:T(1,128)S(1)}, s32[]{:T(128)}, s32[1,1,32]{2,1,0:T(1,128)S(1)}, bf16[10,128,256]{2,1,0:T(8,128)(2,1)}, bf16[32,128,128]{2,1,0:T(8,128)(2,1)}, ...), branch_computations={%region_2.3_spmd, %region_3.4_spmd} | conditional | flops 370411360 | bytes 26219596 | solution.py:105
  100.0 1.8 gather_fusion.1
  101.7 4.0 fusion.19
  105.8 5.5 %copy.18 = f32[32,256,128]{1,0,2:T(8,128)} copy(f32[32,256,128]{2,1,0:T(8,128)} %fusion.19) | data formatting | bytes 8388608 | tf_op jit(solution)/shard_map/while/body/eval_jaxpr/cond/branch_1_fun/sji,sjf->sif/dot_general | solution.py:95
  111.3 3.9 fusion.22
  115.1 1.3 copy.15
  116.5 101.4 %psum.15 = f32[256]{0:T(256)S(1)} all-reduce(f32[256]{0:T(256)S(1)} %get-tuple-element.111), channel_id=1, replica_groups=mesh['row'=128,'col'=4] {'row','col'}, use_global_device_ids=true, to_apply=%region_7.8 | all-reduce | flops 256 | bytes 2048 | tf_op jit(solution)/shard_map/psum | solution.py:123
  218.5 1.9 convolution_bitcast_fusion
  220.4 1.8 convolution_convert_fusion
  222.2 257.6 %all-reduce.2.cloned.1.call-done = f32[256,256]{0,1:T(8,128)} async-done(((f32[256,256]{0,1:T(8,128)}), f32[256,256]{0,1:T(8,128)}) %all-reduce.2.cloned.1.call-update) | async-done | bytes 262160 | tf_op jit(solution)/shard_map/psum | solution.py:123
  479.8 1.0 broadcast_multiply_fusion
  480.8 0.8 copy.16
  (38 shorter events, 5.7 us)
Async XLA Ops:
  7.2 0.9 copy-start
  7.2 16.1 %copy-start.3 = (s32[1,1,32]{2,1,0:T(1,128)S(1)}, s32[1,1,32]{2,1,0:T(1,128)}, u32[]{:S(2)}) copy-start(s32[1,1,32]{2,1,0:T(1,128)} %param.16) | copy-start | bytes 388
  7.2 16.1 %copy-start.4 = (s32[1,1,32]{2,1,0:T(1,128)S(1)}, s32[1,1,32]{2,1,0:T(1,128)}, u32[]{:S(2)}) copy-start(s32[1,1,32]{2,1,0:T(1,128)} %param.17) | copy-start | bytes 388
  7.2 211.2 %reduce-scatter.2.cloned.1.call-start = ((), (), s32[]{:S(2)}) async-start(), calls=%async_computation.1 | async-start | bytes 1310720 | tf_op jit(solution)/shard_map/reduce_scatter | solution.py:113
  40.3 36.8 %copy-start.2 = (bf16[256,256]{1,0:T(8,128)(2,1)S(1)}, bf16[256,256]{1,0:T(8,128)(2,1)}, u32[]{:S(2)}) copy-start(bf16[256,256]{1,0:T(8,128)(2,1)} %param.19) | copy-start | bytes 393220
  40.3 36.8 %copy-start.5 = (f32[256]{0:T(256)S(1)}, f32[256]{0:T(256)}, u32[]{:S(2)}) copy-start(f32[256]{0:T(256)} %param.14) | copy-start | bytes 3076
  40.6 24.9 %collective-permute-start = (f32[2,128,256]{2,0,1:T(2,128)S(1)}, f32[2,128,256]{2,0,1:T(2,128)S(1)}, u32[]{:S(2)}, u32[]{:S(2)}) collective-permute-start(f32[2,128,256]{2,0,1:T(2,128)S(1)} %get-tuple-element.117), channel_id=1, source_target_pairs={{508,0},{0,4},{4,8},{8,12},{12,16},{16,20},{20,24},{24,28},{28,32}... | collective-permute-start | bytes 786440 | tf_op jit(solution)/shard_map/ppermute | solution.py:16
  42.5 23.0 %collective-permute-start.1 = (f32[2,128,256]{2,0,1:T(2,128)S(1)}, f32[2,128,256]{2,0,1:T(2,128)S(1)}, u32[]{:S(2)}, u32[]{:S(2)}) collective-permute-start(f32[2,128,256]{2,0,1:T(2,128)S(1)} %get-tuple-element.120), channel_id=1, source_target_pairs={{4,0},{8,4},{12,8},{16,12},{20,16},{24,20},{28,24},{32,28},{36,32}... | collective-permute-start | bytes 786440 | tf_op jit(solution)/shard_map/ppermute | solution.py:16
  53.6 19.6 %collective-permute-start.2 = (f32[2,128,256]{2,0,1:T(2,128)S(1)}, f32[2,128,256]{2,0,1:T(2,128)S(1)}, u32[]{:S(2)}, u32[]{:S(2)}) collective-permute-start(f32[2,128,256]{2,0,1:T(2,128)S(1)} %get-tuple-element.119), channel_id=1, source_target_pairs={{504,0},{508,4},{0,8},{4,12},{8,16},{12,20},{16,24},{20,28},{24,32... | collective-permute-start | bytes 786440 | tf_op jit(solution)/shard_map/ppermute | solution.py:16
  55.5 21.2 %collective-permute-start.3 = (f32[2,128,256]{2,0,1:T(2,128)S(1)}, f32[2,128,256]{2,0,1:T(2,128)S(1)}, u32[]{:S(2)}, u32[]{:S(2)}) collective-permute-start(f32[2,128,256]{2,0,1:T(2,128)S(1)} %get-tuple-element.118), channel_id=1, source_target_pairs={{8,0},{12,4},{16,8},{20,12},{24,16},{28,20},{32,24},{36,28},{40,32... | collective-permute-start | bytes 786440 | tf_op jit(solution)/shard_map/ppermute | solution.py:16
  77.9 18.0 %collective-permute-start.4 = (bf16[2,128,256]{2,1,0:T(8,128)(2,1)S(1)}, bf16[2,128,256]{2,1,0:T(8,128)(2,1)S(1)}, u32[]{:S(2)}, u32[]{:S(2)}) collective-permute-start(bf16[2,128,256]{2,1,0:T(8,128)(2,1)S(1)} %bitcast.55), channel_id=1, source_target_pairs={{504,0},{508,4},{0,8},{4,12},{8,16},{12,20},{16,24},{20,28},{24,32... | collective-permute-start | bytes 393224 | tf_op jit(solution)/shard_map/ppermute | solution.py:16
  79.8 16.7 %collective-permute-start.5 = (bf16[2,128,256]{2,1,0:T(8,128)(2,1)S(1)}, bf16[2,128,256]{2,1,0:T(8,128)(2,1)S(1)}, u32[]{:S(2)}, u32[]{:S(2)}) collective-permute-start(bf16[2,128,256]{2,1,0:T(8,128)(2,1)S(1)} %bitcast.56), channel_id=1, source_target_pairs={{508,0},{0,4},{4,8},{8,12},{12,16},{16,20},{20,24},{24,28},{28,32}... | collective-permute-start | bytes 393224 | tf_op jit(solution)/shard_map/ppermute | solution.py:16
  81.7 16.1 %collective-permute-start.6 = (bf16[2,128,256]{2,1,0:T(8,128)(2,1)S(1)}, bf16[2,128,256]{2,1,0:T(8,128)(2,1)S(1)}, u32[]{:S(2)}, u32[]{:S(2)}) collective-permute-start(bf16[2,128,256]{2,1,0:T(8,128)(2,1)S(1)} %bitcast.57), channel_id=1, source_target_pairs={{4,0},{8,4},{12,8},{16,12},{20,16},{24,20},{28,24},{32,28},{36,32}... | collective-permute-start | bytes 393224 | tf_op jit(solution)/shard_map/ppermute | solution.py:16
  90.8 7.7 %collective-permute-start.7 = (bf16[2,128,256]{2,1,0:T(8,128)(2,1)S(1)}, bf16[2,128,256]{2,1,0:T(8,128)(2,1)S(1)}, u32[]{:S(2)}, u32[]{:S(2)}) collective-permute-start(bf16[2,128,256]{2,1,0:T(8,128)(2,1)S(1)} %bitcast.58), channel_id=1, source_target_pairs={{8,0},{12,4},{16,8},{20,12},{24,16},{28,20},{32,24},{36,28},{40,32... | collective-permute-start | bytes 393224 | tf_op jit(solution)/shard_map/ppermute | solution.py:16
  115.1 105.2 %copy-start.1 = (bf16[256,256]{1,0:T(8,128)(2,1)S(1)}, bf16[256,256]{1,0:T(8,128)(2,1)}, u32[]{:S(2)}) copy-start(bf16[256,256]{1,0:T(8,128)(2,1)} %param.13) | copy-start | bytes 393220
  116.5 363.3 %all-reduce.2.cloned.1.call-start = ((), (), s32[]{:S(2)}) async-start(), calls=%async_computation.2 | async-start | bytes 524288 | tf_op jit(solution)/shard_map/psum | solution.py:123
Sparse Core Ops, SparseCore 0:
  116.6 26.1 reduce-scatter.1
  220.5 259.2 all-reduce.1
where the time goes:
time: 489 us; the launch traced here: 488 us
  waiting for transfers between devices  269 us (55%)
  blocking collectives  115 us (24%)
  starting transfers between devices  42.9 us (9%)
  local copies, waits for them, and re-layouts  21.8 us (4%)
  matrix products  21.3 us (4%)
  between operations  14.9 us (3%)
    psum x1, waiting for transfers between devices, shards(): lax.psum((weight_term, bias_term), ('row', 'col'))  258 us
    psum x1, blocking collectives, shards(): lax.psum((weight_term, bias_term), ('row', 'col'))  101 us
    ppermute x8, starting transfers between devices, shifted(): return lax.ppermute(block, axis, route)  42.8 us
    all_gather x1, blocking collectives, shards(): lax.all_gather(hidden, 'col', axis=0, tiled=True)  13.2 us
    ppermute x8, waiting for transfers between devices, shifted(): return lax.ppermute(block, axis, route)  11.2 us
  transfers between devices with their start and end apart: 10, of which 3 were waited for; matrix products, arithmetic and copies ran while one was open for 1% of the time, Pallas kernels for 0%

commit v1 on v0

v1 whole, which is shorter than its diff:
```python
import math

import jax
import jax.numpy as jnp
from jax import lax
from jax.experimental import pallas as pl
from jax.experimental.pallas import tpu as pltpu
from jax.sharding import PartitionSpec as P

BLK = 128
HALF = 2
VB = 2
SPAN = 2 * HALF + 1
COLS = 4
ROWS = 128
NY = 8
NZ = 8
MESH = pl.DeviceIdType.MESH
F32 = jnp.float32
BF16 = jnp.bfloat16


def densify(target, source, count, values, dense, wide, first, twice):
    dense[...] = jnp.zeros_like(dense)

    @pl.loop(0, SPAN * VB * COLS * VB)
    def _(cell):
        first[cell] = -1

    @pl.loop(0, count[0, 0])
    def _(slot):
        t = target[0, 0, slot]
        e = source[0, 0, slot]
        cell = t * (COLS * VB) + e
        rows = pl.ds(pl.multiple_of(t * BLK, BLK), BLK)
        lanes = pl.ds(pl.multiple_of(e * BLK, BLK), BLK)
        held = first[cell]

        @pl.when(held < 0)
        def _():
            dense[rows, lanes] = values[0, 0, slot]
            first[cell] = slot
            twice[slot] = 0

        @pl.when(held >= 0)
        def _():
            @pl.when(twice[held] == 0)
            def _():
                wide[held] = values[0, 0, held].astype(F32)
                twice[held] = 1

            wide[held] += values[0, 0, slot].astype(F32)
            dense[rows, lanes] = wide[held].astype(BF16)


def dot(a, b):
    return jnp.dot(a, b, preferred_element_type=F32)


def split(value):
    high = value.astype(BF16)
    return high, (value - high.astype(F32)).astype(BF16)


def layer(
    x_hbm, weight, bias, adj, cot,
    out, grad_in, grad_w, grad_b,
    xg, adj_t, part, part_in, g_all, term, term_in,
    s1_out, s1_in, s2_out, s2_in, s3_buf, s4_buf, s5_buf,
    x_sem, a_send, a_recv, b_send, b_recv, c_send, c_recv, d_send, d_recv, r_send, r_recv,
):
    r = lax.axis_index("row")
    c = lax.axis_index("col")
    z = r // (2 * NY)
    xh = (r // NY) % 2
    y = r % NY
    k = xh * COLS + c
    inner = r % (2 * NY)

    def at_row(distance):
        return (lax.rem(r + distance + ROWS, ROWS), c)

    def at_col(step):
        return (r, lax.rem(c + step, COLS))

    def at_k(other):
        return (z * (2 * NY) + (other // COLS) * NY + y, lax.rem(other, COLS))

    def at_z(other):
        return (other * (2 * NY) + inner, c)

    def at_y(other):
        return (r - y + other, c)

    def ahead(me, step):
        return lax.rem(me + step, 8)

    def send(src, dst, send_sem, recv_sem, device):
        copy = pltpu.make_async_remote_copy(
            src_ref=src, dst_ref=dst, send_sem=send_sem, recv_sem=recv_sem,
            device_id=device, device_id_type=MESH,
        )
        copy.start()
        return copy

    def landed(dst, sem):
        pltpu.make_async_copy(dst, dst, sem).wait()

    own_x = pltpu.make_async_copy(x_hbm, xg.at[c], x_sem)
    own_x.start()
    barrier = pltpu.get_barrier_semaphore()
    for distance in (1, -1, 2, -2):
        pl.semaphore_signal(barrier, inc=1, device_id=at_row(distance), device_id_type=MESH)
    for step in range(1, 8):
        for device in (at_k(ahead(k, step)), at_z(ahead(z, step)), at_y(ahead(y, step))):
            pl.semaphore_signal(barrier, inc=1, device_id=device, device_id_type=MESH)
    pl.semaphore_wait(barrier, 4 + 3 * 7)

    pending = []
    for step in (2, 3, 1):
        pending.append(
            send(x_hbm, xg.at[c], a_send.at[step], a_recv.at[c], at_col(step))
        )

    for i in range(SPAN):
        for j in range(COLS):
            adj_t[j * 256:(j + 1) * 256, i * 256:(i + 1) * 256] = adj[
                i * 256:(i + 1) * 256, j * 256:(j + 1) * 256
            ].T
    own_x.wait()
    for step in (1, 2, 3):
        other = lax.rem(c + step, COLS)
        landed(xg.at[other], a_recv.at[other])

    gathered = xg[...].reshape(COLS * 256, 256)
    for offset in (0, 4, 1, 3):
        part[offset] = dot(adj[offset * 256:(offset + 1) * 256, :], gathered).astype(BF16)
        pending.append(
            send(part.at[offset], part_in.at[offset], b_send.at[offset], b_recv.at[offset], at_row(offset - HALF))
        )
    mixed = dot(adj[HALF * 256:(HALF + 1) * 256, :], gathered)
    for offset in (1, 3, 0, 4):
        landed(part_in.at[offset], b_recv.at[offset])
        mixed += part_in[offset].astype(F32)

    high, low = split(mixed)
    pre = dot(high, weight[...]) + dot(low, weight[...]) + bias[...]
    sig = 1.0 / (1.0 + jnp.exp(-pre))
    exact = cot[...].astype(F32) * (sig * (1.0 + pre * (1.0 - sig)))
    grad = exact.astype(BF16)
    g_all[HALF] = grad
    for offset in (0, 4, 1, 3):
        pending.append(
            send(g_all.at[HALF], g_all.at[offset], c_send.at[offset], c_recv.at[offset], at_row(HALF - offset))
        )
    out[...] = (pre * sig).astype(BF16)

    across = (((0,), (0,)), ((), ()))
    w_term = lax.dot_general(high, grad, across, preferred_element_type=F32) + lax.dot_general(
        low, grad, across, preferred_element_type=F32
    )
    s1_out[...] = w_term.reshape(8, 32, 256)
    for step in range(1, 8):
        other = ahead(k, step)
        pending.append(
            send(s1_out.at[other], s1_in.at[k], r_send.at[0, step], r_recv.at[0, k], at_k(other))
        )
    s1_in[k] = s1_out[k]
    b_term = jnp.sum(exact, axis=0, keepdims=True)
    b_tile = jnp.concatenate([b_term[:, :128], b_term[:, 128:], jnp.zeros((6, 128), F32)], axis=0)

    for step in range(1, 8):
        other = ahead(k, step)
        landed(s1_in.at[other], r_recv.at[0, other])
    total = s1_in[0]
    for i in range(1, 8):
        total += s1_in[i]
    for i in range(8):
        s2_out[i, 0] = total[(i // 2) * 8:(i // 2 + 1) * 8, (i % 2) * 128:(i % 2 + 1) * 128]
        s2_out[i, 1] = b_tile
    for step in range(1, 8):
        other = ahead(z, step)
        pending.append(
            send(s2_out.at[other], s2_in.at[z], r_send.at[1, step], r_recv.at[1, z], at_z(other))
        )
    s2_in[z] = s2_out[z]

    for offset in (1, 3, 0, 4):
        landed(g_all.at[offset], c_recv.at[offset])
    fetched = g_all[...].reshape(SPAN * 256, 256)
    for step in (2, 3, 1):
        other = lax.rem(c + step, COLS)
        rows = pl.ds(pl.multiple_of(other * 256, 256), 256)
        term[step] = dot(adj_t[rows, :], fetched).astype(BF16)
        pending.append(
            send(term.at[step], term_in.at[c], d_send.at[step], d_recv.at[c], at_col(step))
        )
    source = dot(adj_t[pl.ds(pl.multiple_of(c * 256, 256), 256), :], fetched)

    for step in range(1, 8):
        other = ahead(z, step)
        landed(s2_in.at[other], r_recv.at[1, other])
    total = s2_in[0]
    for i in range(1, 8):
        total += s2_in[i]
    s3_buf[y] = total
    for step in range(1, 8):
        other = ahead(y, step)
        pending.append(
            send(s3_buf.at[y], s3_buf.at[y], r_send.at[2, step], r_recv.at[2, y], at_y(other))
        )
    for step in range(1, 8):
        other = ahead(y, step)
        landed(s3_buf.at[other], r_recv.at[2, other])
    total = s3_buf[0]
    for i in range(1, 8):
        total += s3_buf[i]
    total = total * (1.0 / math.sqrt(256 * ROWS * COLS))
    s4_buf[z] = total[0]
    for step in range(1, 8):
        other = ahead(z, step)
        pending.append(
            send(s4_buf.at[z], s4_buf.at[z], r_send.at[3, step], r_recv.at[3, z], at_z(other))
        )
    s5_buf[k, 8] = total[1]

    for step in (1, 2, 3):
        other = lax.rem(c + step, COLS)
        landed(term_in.at[other], d_recv.at[other])
        source += term_in[other].astype(F32)
    grad_in[...] = lax.dot_general(
        source.astype(BF16), weight[...], (((1,), (1,)), ((), ())), preferred_element_type=F32
    ).astype(BF16)

    for step in range(1, 8):
        other = ahead(z, step)
        landed(s4_buf.at[other], r_recv.at[3, other])
    for i in range(8):
        s5_buf[k, i] = s4_buf[i]
    for step in range(1, 8):
        other = ahead(k, step)
        pending.append(
            send(s5_buf.at[k], s5_buf.at[k], r_send.at[4, step], r_recv.at[4, k], at_k(other))
        )
    for step in range(1, 8):
        other = ahead(k, step)
        landed(s5_buf.at[other], r_recv.at[4, other])
    b_sum = s5_buf[0, 8]
    for i in range(1, 8):
        b_sum += s5_buf[i, 8]
    for i in range(8):
        for j in range(8):
            grad_w[i * 32 + (j // 2) * 8:i * 32 + (j // 2 + 1) * 8, (j % 2) * 128:(j % 2 + 1) * 128] = s5_buf[i, j]
    grad_b[:, :128] = b_sum[0:1]
    grad_b[:, 128:] = b_sum[1:2]
    for copy in pending:
        copy.wait_send()


def shards(
    features, weight, bias, block_values, block_target, block_source, block_count, cotangent
):
    slots = block_values.shape[2]
    vmem = pl.BlockSpec(memory_space=pltpu.VMEM)
    smem = pl.BlockSpec(memory_space=pltpu.SMEM)
    adjacency = pl.pallas_call(
        densify,
        out_shape=jax.ShapeDtypeStruct((SPAN * VB * BLK, COLS * VB * BLK), BF16),
        in_specs=[smem, smem, smem, vmem],
        out_specs=vmem,
        scratch_shapes=[
            pltpu.VMEM((slots, BLK, BLK), F32),
            pltpu.SMEM((SPAN * VB * COLS * VB,), jnp.int32),
            pltpu.SMEM((slots,), jnp.int32),
        ],
        compiler_params=pltpu.CompilerParams(vmem_limit_bytes=16 << 20),
        name="densify",
    )(block_target, block_source, block_count, block_values)

    dma = pltpu.SemaphoreType.DMA
    output, grad_inputs, grad_weight, grad_bias = pl.pallas_call(
        layer,
        out_shape=(
            jax.ShapeDtypeStruct((256, 256), BF16),
            jax.ShapeDtypeStruct((256, 256), BF16),
            jax.ShapeDtypeStruct((256, 256), F32),
            jax.ShapeDtypeStruct((1, 256), F32),
        ),
        in_specs=[pl.BlockSpec(memory_space=pl.ANY), vmem, vmem, vmem, vmem],
        out_specs=(vmem, vmem, vmem, vmem),
        scratch_shapes=[
            pltpu.VMEM((COLS, 256, 256), BF16),
            pltpu.VMEM((COLS * 256, SPAN * 256), BF16),
            pltpu.VMEM((SPAN, 256, 256), BF16),
            pltpu.VMEM((SPAN, 256, 256), BF16),
            pltpu.VMEM((SPAN, 256, 256), BF16),
            pltpu.VMEM((COLS, 256, 256), BF16),
            pltpu.VMEM((COLS, 256, 256), BF16),
            pltpu.VMEM((8, 32, 256), F32),
            pltpu.VMEM((8, 32, 256), F32),
            pltpu.VMEM((8, 2, 8, 128), F32),
            pltpu.VMEM((8, 2, 8, 128), F32),
            pltpu.VMEM((8, 2, 8, 128), F32),
            pltpu.VMEM((8, 8, 128), F32),
            pltpu.VMEM((8, 9, 8, 128), F32),
            dma,
            dma((COLS,)),
            dma((COLS,)),
            dma((SPAN,)),
            dma((SPAN,)),
            dma((SPAN,)),
            dma((SPAN,)),
            dma((COLS,)),
            dma((COLS,)),
            dma((5, 8)),
            dma((5, 8)),
        ],
        compiler_params=pltpu.CompilerParams(
            collective_id=0, has_side_effects=True, vmem_limit_bytes=32 << 20
        ),
        name="layer",
    )(features, weight, bias.reshape(1, 256), adjacency, cotangent)
    return output, grad_inputs, grad_weight, grad_bias.reshape(256)


def solution(mesh):
    return jax.shard_map(
        shards,
        mesh=mesh,
        in_specs=(
            P(("row", "col"), None),
            P(),
            P(),
            P("row", "col", None, None, None),
            P("row", "col", None),
            P("row", "col", None),
            P("row", "col"),
            P(("row", "col"), None),
        ),
        out_specs=(P(("row", "col"), None), P(("row", "col"), None), P(), P()),
        check_vma=False,
    )
```

time: 489 us -> 72.1 us (0.15)
  waiting for transfers between devices: 269 us -> 0 us
  blocking collectives: 115 us -> 0 us
  Pallas kernels: 0 us -> 65.4 us
  starting transfers between devices: 42.9 us -> 0 us
  matrix products: 21.3 us -> 0 us
  local copies, waits for them, and re-layouts: 21.8 us -> 5.12 us
  between operations: 14.9 us -> 1.36 us
    psum x1 -> x0, waiting for transfers between devices: 258 us -> none  [shards(): lax.psum((weight_term, bias_term), ('row', 'col'))]
    psum x1 -> x0, blocking collectives: 101 us -> none  [shards(): lax.psum((weight_term, bias_term), ('row', 'col'))]
    pallas_call x0 -> x2, Pallas kernels: none -> 65.4 us  [the longest x1 63.6 us: shards(): pl.pallas_call(layer, out_shape=(jax.ShapeDtypeStruct((256, 256), BF16),...]
    ppermute x8 -> x0, starting transfers between devices: 42.8 us -> none  [shifted(): return lax.ppermute(block, axis, route)]
    dot_general x7 -> x0, matrix products: 21.3 us -> none  [the longest x1 4.65 us: forward_add_group(): jnp.einsum('sij,sjf->sif', block_part, picked, preferred_element_type=jnp...]
    all_gather x1 -> x0, blocking collectives: 13.2 us -> none  [shards(): lax.all_gather(hidden, 'col', axis=0, tiled=True)]
    ppermute x8 -> x0, waiting for transfers between devices: 11.2 us -> none  [shifted(): return lax.ppermute(block, axis, route)]
    dot_general x2 -> x0, local copies, waits for them, and re-layouts: 11 us -> none  [the longest x1 5.51 us: forward_add_group(): jnp.einsum('sij,sjf->sif', block_part, picked, preferred_element_type=jnp...]
  transfers between devices with their start and end apart: 10 -> 0, of which waited for: 3 -> 0; matrix products, arithmetic and copies ran while one was open for 1% -> 0% of each run, Pallas kernels for 0% -> 0%
where the time goes in v1:
time: 72.1 us; the launch traced here: 71.9 us
  Pallas kernels  65.4 us (91%)
  local copies, waits for them, and re-layouts  5.12 us (7%)
  between operations  1.36 us (2%)
    pallas_call x1, Pallas kernels, shards(): pl.pallas_call(layer, out_shape=(jax.ShapeDtypeStruct((256, 256), BF16),...  63.6 us
    unnamed x18, local copies, waits for them, and re-layouts  5.12 us
    pallas_call x1, Pallas kernels, shards(): pl.pallas_call(densify, out_shape=jax.ShapeDtypeStruct((SPAN * VB * BLK,...  1.84 us

profile of v1, /device:TPU:1, one launch (start us, length us, event | category | flops | bytes accessed | tf_op | source)
XLA Modules:
  0.0 71.9 jit_solution(13674480721318901994)
XLA Ops:
  0.6 0.0 copy-start.4
  1.3 0.0 copy-start
  1.3 1.2 %copy-done = bf16[1,1,32,128,128]{4,3,2,1,0:T(8,128)(2,1)S(1)} copy-done((bf16[1,1,32,128,128]{4,3,2,1,0:T(8,128)(2,1)S(1)}, bf16[1,1,32,128,128]{4,3,2,1,0:T(8,128)(2,1)}, u32[]{:S(2)}) %copy-start) | copy-done | bytes 1048600
  2.5 0.0 copy-start.5
  2.5 0.7 copy-done.5
  3.2 0.0 copy-start.6
  3.2 0.7 copy-done.6
  3.8 0.0 copy-start.1
  3.8 0.0 copy-start.2
  3.8 0.0 copy-start.3
  3.8 1.8 %densify.1.adj = bf16[1280,1024]{1,0:T(8,128)(2,1)S(1)} custom-call(s32[1,1,32]{2,1,0:T(1,128)S(1)} %copy-done.5, s32[1,1,32]{2,1,0:T(1,128)S(1)} %copy-done.6, s32[1,1]{1,0:T(1,128)S(6)} %copy.16.count, bf16[1,1,32,128,128]{4,3,2,1,0:T(8,128)(2,1)S(1)} %copy-done), custom_call_target="tpu_custom_call" | custom-call | tf_op jit(solution)/shard_map/densify/pallas_call | solution.py:266
  5.7 0.0 copy-done.4
  5.7 0.0 copy-done.1
  5.7 0.0 copy-done.2
  5.7 0.0 copy-done.3
  5.7 63.6 %layer.1 = (bf16[256,256]{1,0:T(8,128)(2,1)S(1)}, bf16[256,256]{1,0:T(8,128)(2,1)S(1)}, f32[256,256]{1,0:T(8,128)S(1)}, f32[1,256]{1,0:T(1,128)S(1)}) custom-call(bf16[256,256]{1,0:T(8,128)(2,1)S(1)} %copy-done.1, bf16[256,256]{1,0:T(8,128)(2,1)S(1)} %copy-done.2, f32[1,256]{1,0:T(1,128)S(1)} %bitcast.2, bf16[1280,1024]{1,0:T(8,128)(2,1)S(1)} %densify.1.adj, ...), custom_call_target="tpu_custom_call" | custom-call | tf_op jit(solution)/shard_map/layer/pallas_call | solution.py:281
  69.3 0.7 copy.17
  70.0 0.7 copy.18
  70.7 0.7 copy.19
  71.4 0.6 copy.20
Async XLA Ops:
  0.6 5.1 %copy-start.4 = (f32[256]{0:T(256)S(1)}, f32[256]{0:T(256)}, u32[]{:S(2)}) copy-start(f32[256]{0:T(256)} %param.10) | copy-start | bytes 3076
  1.3 1.2 %copy-start = (bf16[1,1,32,128,128]{4,3,2,1,0:T(8,128)(2,1)S(1)}, bf16[1,1,32,128,128]{4,3,2,1,0:T(8,128)(2,1)}, u32[]{:S(2)}) copy-start(bf16[1,1,32,128,128]{4,3,2,1,0:T(8,128)(2,1)} %values.1) | copy-start | bytes 3145732
  2.5 0.7 copy-start.5
  3.2 0.7 copy-start.6
  3.8 1.9 %copy-start.1 = (bf16[256,256]{1,0:T(8,128)(2,1)S(1)}, bf16[256,256]{1,0:T(8,128)(2,1)}, u32[]{:S(2)}) copy-start(bf16[256,256]{1,0:T(8,128)(2,1)} %x_hbm.1) | copy-start | bytes 393220
  3.8 1.9 %copy-start.2 = (bf16[256,256]{1,0:T(8,128)(2,1)S(1)}, bf16[256,256]{1,0:T(8,128)(2,1)}, u32[]{:S(2)}) copy-start(bf16[256,256]{1,0:T(8,128)(2,1)} %weight.1) | copy-start | bytes 393220
  3.8 1.9 %copy-start.3 = (bf16[256,256]{1,0:T(8,128)(2,1)S(1)}, bf16[256,256]{1,0:T(8,128)(2,1)}, u32[]{:S(2)}) copy-start(bf16[256,256]{1,0:T(8,128)(2,1)} %cot.1) | copy-start | bytes 393220

commit v2 on v1

v2 whole, which is shorter than its diff:
```python
import math

import jax
import jax.numpy as jnp
from jax import lax
from jax.experimental import pallas as pl
from jax.experimental.pallas import tpu as pltpu
from jax.sharding import PartitionSpec as P

BLK = 128
HALF = 2
VB = 2
SPAN = 2 * HALF + 1
COLS = 4
ROWS = 128
NY = 8
NZ = 8
SLOTS = 32
VMEM_BYTES = 63 << 20
CELLS = SPAN * VB * COLS * VB
MESH = pl.DeviceIdType.MESH
F32 = jnp.float32
BF16 = jnp.bfloat16


def dot(a, b):
    return jnp.dot(a, b, preferred_element_type=F32)


def split(value):
    high = value.astype(BF16)
    return high, (value - high.astype(F32)).astype(BF16)


def layer(
    x_hbm, weight_hbm, bias_hbm, values_hbm, target_hbm, source_hbm, count_hbm, cot_hbm,
    out_hbm, grad_in_hbm, grad_w_hbm, grad_b_hbm,
    out, grad_in, grad_w, grad_b, weight, bias, cot, values, target, source_of, count, table_v, table, wide, adj, fwd,
    xg, adj_t, part, part_in, g_all, term, term_in,
    w_own, w_out, w_in, w_z, w_y, w_k, bias_k, bias_z, bias_y,
    in_sem, a_send, a_recv, b_send, b_recv, c_send, c_recv, d_send, d_recv, r_send, r_recv,
):
    r = lax.axis_index("row")
    c = lax.axis_index("col")
    z = r // (2 * NY)
    xh = (r // NY) % 2
    y = r % NY
    k = xh * COLS + c
    inner = r % (2 * NY)

    def at_row(distance):
        return (lax.rem(r + distance + ROWS, ROWS), c)

    def at_col(step):
        return (r, lax.rem(c + step, COLS))

    def at_k(other):
        return (z * (2 * NY) + (other // COLS) * NY + y, lax.rem(other, COLS))

    def at_z(other):
        return (other * (2 * NY) + inner, c)

    def at_y(other):
        return (r - y + other, c)

    def ahead(me, step):
        return lax.rem(me + step, 8)

    def send(src, dst, send_sem, recv_sem, device):
        copy = pltpu.make_async_remote_copy(
            src_ref=src, dst_ref=dst, send_sem=send_sem, recv_sem=recv_sem,
            device_id=device, device_id_type=MESH,
        )
        copy.start()
        return copy

    def landed(dst, sem):
        pltpu.make_async_copy(dst, dst, sem).wait()

    def total_of(parts):
        total = parts[0].astype(F32)
        for i in range(1, 8):
            total += parts[i].astype(F32)
        return total

    def local(i, src, dst):
        copy = pltpu.make_async_copy(src, dst, in_sem.at[i])
        copy.start()
        return copy

    barrier = pltpu.get_barrier_semaphore()
    for step in range(1, 8):
        for device in (at_k(ahead(k, step)), at_z(ahead(z, step)), at_y(ahead(y, step))):
            pl.semaphore_signal(barrier, inc=1, device_id=device, device_id_type=MESH)
    for distance in (1, -1, 2, -2):
        pl.semaphore_signal(barrier, inc=1, device_id=at_row(distance), device_id_type=MESH)
    scalars = [
        local(0, target_hbm, target),
        local(1, source_hbm, source_of),
        local(2, count_hbm, count),
    ]
    own_x = local(3, x_hbm, xg.at[c])
    values_in = local(4, values_hbm, values)
    late = [local(5, weight_hbm, weight), local(6, bias_hbm, bias), local(7, cot_hbm, cot)]
    pl.semaphore_wait(barrier, 4 + 3 * 7)
    pending = []
    sibling = c + 1 - 2 * lax.rem(c, 2)
    facing = lax.rem(c + 2, COLS)
    behind = lax.rem(sibling + 2, COLS)
    halves = (pl.ds(0, 128), pl.ds(128, 128))
    for i, rows in enumerate(halves):
        pending.append(
            send(x_hbm.at[rows], xg.at[c, rows], a_send.at[i], a_recv.at[i], (r, facing))
        )
    pending.append(send(x_hbm, xg.at[c], a_send.at[2], a_recv.at[2], (r, sibling)))
    for copy in scalars:
        copy.wait()
    lane = lax.broadcasted_iota(jnp.int32, (SLOTS, 128), 1)
    sub = lax.broadcasted_iota(jnp.int32, (SLOTS, 128), 0)
    in_row = jnp.full((SLOTS, 128), CELLS, jnp.int32)
    in_col = jnp.full((SLOTS, 128), CELLS, jnp.int32)
    for slot in range(SLOTS):
        cell = jnp.where(
            slot < count[0, 0], target[0, 0, slot] * (COLS * VB) + source_of[0, 0, slot], CELLS
        )
        in_row = jnp.where(lane == slot, cell, in_row)
        in_col = jnp.where(sub == slot, cell, in_col)
    table_v[0:1, :] = jnp.min(jnp.where(in_col == lane, sub, SLOTS), axis=0, keepdims=True)
    table_v[1:2, :] = jnp.min(
        jnp.where((in_col == in_row) & (sub > lane), sub, SLOTS), axis=0, keepdims=True
    )
    tabled = local(8, table_v, table)
    tabled.wait()
    values_in.wait()
    wide[SLOTS] = jnp.zeros((BLK, BLK), F32)
    for slot in range(SLOTS - 1, -1, -1):
        wide[slot] = values[0, 0, slot].astype(F32) + wide[table[1, slot]]
    for d in range(SPAN * VB):
        for e in range(COLS * VB):
            block = wide[table[0, d * (COLS * VB) + e]].astype(BF16)
            adj[d * BLK:(d + 1) * BLK, e * BLK:(e + 1) * BLK] = block
            adj_t[e * BLK:(e + 1) * BLK, d * BLK:(d + 1) * BLK] = block.T
    for i, rows in enumerate(halves):
        landed(xg.at[facing, rows], a_recv.at[i])
        pending.append(
            send(xg.at[facing, rows], xg.at[facing, rows], a_send.at[3 + i], a_recv.at[3 + i], (r, sibling))
        )
    own_x.wait()
    landed(xg.at[sibling], a_recv.at[2])
    for copy in late:
        copy.wait()
    chip = c // 2
    near = xg[pl.ds(2 * chip, 2)].reshape(512, 256)
    near_lanes = pl.ds(pl.multiple_of(chip * 512, 512), 512)
    for offset in (0, 4, 1, 3, 2):
        fwd[offset] = dot(adj[offset * 256:(offset + 1) * 256, near_lanes], near)
    for i, rows in enumerate(halves):
        landed(xg.at[behind, rows], a_recv.at[3 + i])
    far = xg[pl.ds(2 - 2 * chip, 2)].reshape(512, 256)
    far_lanes = pl.ds(pl.multiple_of(512 - chip * 512, 512), 512)
    for offset in (0, 4, 1, 3):
        part[offset] = (
            fwd[offset] + dot(adj[offset * 256:(offset + 1) * 256, far_lanes], far)
        ).astype(BF16)
        pending.append(
            send(part.at[offset], part_in.at[offset], b_send.at[offset], b_recv.at[offset], at_row(offset - HALF))
        )
    mixed = fwd[HALF] + dot(adj[HALF * 256:(HALF + 1) * 256, far_lanes], far)
    for offset in (1, 3, 0, 4):
        landed(part_in.at[offset], b_recv.at[offset])
        mixed += part_in[offset].astype(F32)

    high, low = split(mixed)
    pre = dot(high, weight[...]) + dot(low, weight[...]) + bias[...]
    sig = 1.0 / (1.0 + jnp.exp(-pre))
    exact = cot[...].astype(F32) * (sig * (1.0 + pre * (1.0 - sig)))
    grad = exact.astype(BF16)
    g_all[HALF] = grad
    for offset in (0, 4, 1, 3):
        pending.append(
            send(g_all.at[HALF], g_all.at[offset], c_send.at[offset], c_recv.at[offset], at_row(HALF - offset))
        )
    out[...] = (pre * sig).astype(BF16)

    written = [local(9, out, out_hbm)]
    across = (((0,), (0,)), ((), ()))
    w_term = lax.dot_general(high, grad, across, preferred_element_type=F32) + lax.dot_general(
        low, grad, across, preferred_element_type=F32
    )
    w_own[...] = w_term.reshape(8, 32, 256)
    w_out[...] = w_term.reshape(8, 32, 256).astype(BF16)
    bias_k[k] = jnp.sum(exact, axis=0, keepdims=True)
    for step in range(1, 8):
        other = ahead(k, step)
        pending.append(
            send(w_out.at[other], w_in.at[k], r_send.at[0, step], r_recv.at[0, k], at_k(other))
        )
        pending.append(
            send(bias_k.at[k], bias_k.at[k], r_send.at[1, step], r_recv.at[1, k], at_k(other))
        )
    w_in[k] = jnp.zeros((32, 256), BF16)
    for step in range(1, 8):
        other = ahead(k, step)
        landed(w_in.at[other], r_recv.at[0, other])
        landed(bias_k.at[other], r_recv.at[1, other])
    w_z[z] = (w_own[k] + total_of(w_in)).astype(BF16)
    bias_z[z] = total_of(bias_k)
    for step in range(1, 8):
        other = ahead(z, step)
        pending.append(
            send(w_z.at[z], w_z.at[z], r_send.at[2, step], r_recv.at[2, z], at_z(other))
        )
        pending.append(
            send(bias_z.at[z], bias_z.at[z], r_send.at[3, step], r_recv.at[3, z], at_z(other))
        )
    for step in range(1, 8):
        other = ahead(z, step)
        landed(w_z.at[other], r_recv.at[2, other])
        landed(bias_z.at[other], r_recv.at[3, other])
    w_y[y] = total_of(w_z).astype(BF16)
    bias_y[y] = total_of(bias_z)
    for step in range(1, 8):
        other = ahead(y, step)
        pending.append(
            send(w_y.at[y], w_y.at[y], r_send.at[4, step], r_recv.at[4, y], at_y(other))
        )
        pending.append(
            send(bias_y.at[y], bias_y.at[y], r_send.at[5, step], r_recv.at[5, y], at_y(other))
        )
    for offset in (1, 3, 0, 4):
        landed(g_all.at[offset], c_recv.at[offset])
    fetched = g_all[...].reshape(SPAN * 256, 256)
    for step in (2, 3, 1):
        other = lax.rem(c + step, COLS)
        rows = pl.ds(pl.multiple_of(other * 256, 256), 256)
        term[step] = dot(adj_t[rows, :], fetched).astype(BF16)
        pending.append(
            send(term.at[step], term_in.at[c], d_send.at[step], d_recv.at[c], at_col(step))
        )
    source = dot(adj_t[pl.ds(pl.multiple_of(c * 256, 256), 256), :], fetched)
    for step in range(1, 8):
        other = ahead(y, step)
        landed(w_y.at[other], r_recv.at[4, other])
        landed(bias_y.at[other], r_recv.at[5, other])
    normalizer = 1.0 / math.sqrt(256 * ROWS * COLS)
    w_k[k] = (total_of(w_y) * normalizer).astype(BF16)
    for step in range(1, 8):
        other = ahead(k, step)
        pending.append(
            send(w_k.at[k], w_k.at[k], r_send.at[6, step], r_recv.at[6, k], at_k(other))
        )
    grad_b[...] = total_of(bias_y) * normalizer
    written.append(local(10, grad_b, grad_b_hbm))
    for step in (1, 2, 3):
        other = lax.rem(c + step, COLS)
        landed(term_in.at[other], d_recv.at[other])
        source += term_in[other].astype(F32)
    grad_in[...] = lax.dot_general(
        source.astype(BF16), weight[...], (((1,), (1,)), ((), ())), preferred_element_type=F32
    ).astype(BF16)
    written.append(local(11, grad_in, grad_in_hbm))
    for step in range(1, 8):
        other = ahead(k, step)
        landed(w_k.at[other], r_recv.at[6, other])
    grad_w[...] = w_k[...].astype(F32).reshape(256, 256)
    written.append(local(12, grad_w, grad_w_hbm))
    for copy in pending:
        copy.wait_send()
    for copy in written:
        copy.wait()


def hand_over(*refs):
    sems = refs[-1]
    n = (len(refs) - 1) // 3
    for i in range(n):
        pltpu.make_async_copy(refs[i], refs[2 * n + i], sems.at[0, i]).start()
    for i in range(n):
        pltpu.make_async_copy(refs[i], refs[2 * n + i], sems.at[0, i]).wait()
        pltpu.make_async_copy(refs[2 * n + i], refs[n + i], sems.at[1, i]).start()
    for i in range(n):
        pltpu.make_async_copy(refs[2 * n + i], refs[n + i], sems.at[1, i]).wait()


def shards(
    features, weight, bias, block_values, block_target, block_source, block_count, cotangent
):
    hbm = pl.BlockSpec(memory_space=pltpu.HBM)
    dma = pltpu.SemaphoreType.DMA
    shapes = (
        jax.ShapeDtypeStruct((256, 256), BF16),
        jax.ShapeDtypeStruct((256, 256), BF16),
        jax.ShapeDtypeStruct((256, 256), F32),
        jax.ShapeDtypeStruct((1, 256), F32),
    )
    staged = [pltpu.VMEM(leaf.shape, leaf.dtype) for leaf in shapes]
    results = pl.pallas_call(
        layer,
        out_shape=shapes,
        in_specs=[hbm] * 8,
        out_specs=(hbm,) * 4,
        scratch_shapes=[
            *staged,
            pltpu.VMEM((256, 256), BF16),
            pltpu.VMEM((1, 256), F32),
            pltpu.VMEM((256, 256), BF16),
            pltpu.VMEM((1, 1, SLOTS, BLK, BLK), BF16),
            pltpu.SMEM((1, 1, SLOTS), jnp.int32),
            pltpu.SMEM((1, 1, SLOTS), jnp.int32),
            pltpu.SMEM((1, 1), jnp.int32),
            pltpu.VMEM((2, 128), jnp.int32),
            pltpu.SMEM((2, 128), jnp.int32),
            pltpu.VMEM((SLOTS + 1, BLK, BLK), F32),
            pltpu.VMEM((SPAN * 256, COLS * 256), BF16),
            pltpu.VMEM((SPAN, 256, 256), F32),
            pltpu.VMEM((COLS, 256, 256), BF16),
            pltpu.VMEM((COLS * 256, SPAN * 256), BF16),
            pltpu.VMEM((SPAN, 256, 256), BF16),
            pltpu.VMEM((SPAN, 256, 256), BF16),
            pltpu.VMEM((SPAN, 256, 256), BF16),
            pltpu.VMEM((COLS, 256, 256), BF16),
            pltpu.VMEM((COLS, 256, 256), BF16),
            pltpu.VMEM((8, 32, 256), F32),
            pltpu.VMEM((8, 32, 256), BF16),
            pltpu.VMEM((8, 32, 256), BF16),
            pltpu.VMEM((8, 32, 256), BF16),
            pltpu.VMEM((8, 32, 256), BF16),
            pltpu.VMEM((8, 32, 256), BF16),
            pltpu.VMEM((8, 1, 256), F32),
            pltpu.VMEM((8, 1, 256), F32),
            pltpu.VMEM((8, 1, 256), F32),
            dma((13,)),
            dma((5,)),
            dma((5,)),
            dma((SPAN,)),
            dma((SPAN,)),
            dma((SPAN,)),
            dma((SPAN,)),
            dma((COLS,)),
            dma((COLS,)),
            dma((7, 8)),
            dma((7, 8)),
        ],
        compiler_params=pltpu.CompilerParams(
            collective_id=0, has_side_effects=True, vmem_limit_bytes=VMEM_BYTES
        ),
        name="layer",
    )(
        features, weight, bias.reshape(1, 256), block_values, block_target, block_source, block_count, cotangent
    )
    output, grad_inputs, grad_weight, grad_bias = pl.pallas_call(
        hand_over,
        out_shape=shapes,
        in_specs=[hbm] * 4,
        out_specs=(hbm,) * 4,
        scratch_shapes=[*staged, dma((2, 4))],
        compiler_params=pltpu.CompilerParams(vmem_limit_bytes=VMEM_BYTES),
        name="hand_over",
    )(*results)
    return output, grad_inputs, grad_weight, grad_bias.reshape(256)


def solution(mesh):
    return jax.shard_map(
        shards,
        mesh=mesh,
        in_specs=(
            P(("row", "col"), None),
            P(),
            P(),
            P("row", "col", None, None, None),
            P("row", "col", None),
            P("row", "col", None),
            P("row", "col"),
            P(("row", "col"), None),
        ),
        out_specs=(P(("row", "col"), None), P(("row", "col"), None), P(), P()),
        check_vma=False,
    )
```

time: 72.1 us -> 65.5 us (0.908)
  local copies, waits for them, and re-layouts: 5.12 us -> 0 us
  Pallas kernels: 65.4 us -> 64.1 us
    unnamed x18 -> x0, local copies, waits for them, and re-layouts: 5.12 us -> none
    pallas_call x2, Pallas kernels: 65.4 us -> 64.1 us  [the longest x1 62.2 us: shards(): pl.pallas_call(layer, out_shape=shapes, in_specs=[hbm] * 8, out_specs=(hb...]
where the time goes in v2:
time: 65.5 us; the launch traced here: 65.4 us
  Pallas kernels  64.1 us (98%)
  between operations  1.29 us (2%)
    pallas_call x1, Pallas kernels, shards(): pl.pallas_call(layer, out_shape=shapes, in_specs=[hbm] * 8, out_specs=(hb...  62.2 us
    pallas_call x1, Pallas kernels, shards(): pl.pallas_call(hand_over, out_shape=shapes, in_specs=[hbm] * 4, out_specs...  1.86 us

profile of v2, /device:TPU:1, one launch (start us, length us, event | category | flops | bytes accessed | tf_op | source)
XLA Modules:
  0.0 65.4 jit_solution(10480134006430405306)
XLA Ops:
  1.3 62.2 %layer.1 = (bf16[256,256]{1,0:T(8,128)(2,1)}, bf16[256,256]{1,0:T(8,128)(2,1)}, f32[256,256]{1,0:T(8,128)}, f32[1,256]{1,0:T(1,128)}) custom-call(bf16[256,256]{1,0:T(8,128)(2,1)} %x_hbm.1, bf16[256,256]{1,0:T(8,128)(2,1)} %weight_hbm.1, f32[1,256]{1,0:T(1,128)} %bitcast.2, bf16[1,1,32,128,128]{4,3,2,1,0:T(8,128)(2,1)} %values_hbm.1, ...), custom_call_target="tpu_custom_call" | custom-call | tf_op jit(solution)/shard_map/layer/pallas_call | solution.py:297
  63.5 1.9 %hand_over.1 = (bf16[256,256]{1,0:T(8,128)(2,1)}, bf16[256,256]{1,0:T(8,128)(2,1)}, f32[256,256]{1,0:T(8,128)}, f32[1,256]{1,0:T(1,128)}) custom-call(bf16[256,256]{1,0:T(8,128)(2,1)} %get-tuple-element.12.refs_0_, bf16[256,256]{1,0:T(8,128)(2,1)} %get-tuple-element.13.refs_1_, f32[256,256]{1,0:T(8,128)} %get-tuple-element.14.refs_2_, ...), custom_call_target="tpu_custom_call" | custom-call | tf_op jit(solution)/shard_map/hand_over/pallas_call | solution.py:351

commit v3 on v2

v3 whole, which is shorter than its diff:
```python
import math

import jax
import jax.numpy as jnp
from jax import lax
from jax.experimental import pallas as pl
from jax.experimental.pallas import tpu as pltpu
from jax.sharding import PartitionSpec as P

BLK = 128
HALF = 2
VB = 2
SPAN = 2 * HALF + 1
COLS = 4
ROWS = 128
NY = 8
NZ = 8
SLOTS = 32
VMEM_BYTES = 54810 << 10
CELLS = SPAN * VB * COLS * VB
MESH = pl.DeviceIdType.MESH
F32 = jnp.float32
BF16 = jnp.bfloat16


def dot(a, b):
    return jnp.dot(a, b, preferred_element_type=F32)


def split(value):
    high = value.astype(BF16)
    return high, (value - high.astype(F32)).astype(BF16)


def layer(
    x_hbm, weight_hbm, bias_hbm, values_hbm, target_hbm, source_hbm, count_hbm, cot_hbm,
    out, grad_in, grad_w, grad_b,
    weight, bias, cot, values, target, source_of, count, table_v, table, wide, adj, fwd, bwd,
    xg, adj_t, part, part_in, g_all, term, term_in,
    w_own, w_out, w_in, w_z, w_y, w_k, bias_k, bias_z, bias_y,
    in_sem, a_send, a_recv, b_send, b_recv, c_send, c_recv, d_send, d_recv, r_send, r_recv,
):
    r = lax.axis_index("row")
    c = lax.axis_index("col")
    z = r // (2 * NY)
    xh = (r // NY) % 2
    y = r % NY
    k = xh * COLS + c
    inner = r % (2 * NY)

    def at_row(distance):
        return (lax.rem(r + distance + ROWS, ROWS), c)

    def at_col(step):
        return (r, lax.rem(c + step, COLS))

    def at_k(other):
        return (z * (2 * NY) + (other // COLS) * NY + y, lax.rem(other, COLS))

    def at_z(other):
        return (other * (2 * NY) + inner, c)

    def at_y(other):
        return (r - y + other, c)

    def ahead(me, step):
        return lax.rem(me + step, 8)

    def send(src, dst, send_sem, recv_sem, device):
        copy = pltpu.make_async_remote_copy(
            src_ref=src, dst_ref=dst, send_sem=send_sem, recv_sem=recv_sem,
            device_id=device, device_id_type=MESH,
        )
        copy.start()

    def landed(dst, sem):
        pltpu.make_async_copy(dst, dst, sem).wait()

    def total_of(parts):
        total = parts[0].astype(F32)
        for i in range(1, 8):
            total += parts[i].astype(F32)
        return total

    def local(i, src, dst):
        copy = pltpu.make_async_copy(src, dst, in_sem.at[i])
        copy.start()
        return copy

    barrier = pltpu.get_barrier_semaphore()
    for step in range(1, 8):
        for device in (at_k(ahead(k, step)), at_z(ahead(z, step)), at_y(ahead(y, step))):
            pl.semaphore_signal(barrier, inc=1, device_id=device, device_id_type=MESH)
    for distance in (1, -1, 2, -2):
        pl.semaphore_signal(barrier, inc=1, device_id=at_row(distance), device_id_type=MESH)
    scalars = [
        local(0, target_hbm, target),
        local(1, source_hbm, source_of),
        local(2, count_hbm, count),
    ]
    own_x = local(3, x_hbm, xg.at[c])
    values_in = local(4, values_hbm, values)
    late = [local(5, weight_hbm, weight), local(6, bias_hbm, bias), local(7, cot_hbm, cot)]
    pl.semaphore_wait(barrier, 4 + 3 * 7)
    sibling = c + 1 - 2 * lax.rem(c, 2)
    facing = lax.rem(c + 2, COLS)
    behind = lax.rem(sibling + 2, COLS)
    pieces = [pl.ds(64 * i, 64) for i in range(4)]
    for i, rows in enumerate(pieces):
        send(x_hbm.at[rows], xg.at[c, rows], a_send, a_recv.at[i], (r, facing)
        )
    send(x_hbm, xg.at[c], a_send, a_recv.at[4], (r, sibling))
    for copy in scalars:
        copy.wait()
    lane = lax.broadcasted_iota(jnp.int32, (SLOTS, 128), 1)
    sub = lax.broadcasted_iota(jnp.int32, (SLOTS, 128), 0)
    in_row = jnp.full((SLOTS, 128), CELLS, jnp.int32)
    in_col = jnp.full((SLOTS, 128), CELLS, jnp.int32)
    for slot in range(SLOTS):
        cell = jnp.where(
            slot < count[0, 0], target[0, 0, slot] * (COLS * VB) + source_of[0, 0, slot], CELLS
        )
        in_row = jnp.where(lane == slot, cell, in_row)
        in_col = jnp.where(sub == slot, cell, in_col)
    table_v[0:1, :] = jnp.min(jnp.where(in_col == lane, sub, SLOTS), axis=0, keepdims=True)
    table_v[1:2, :] = jnp.min(
        jnp.where((in_col == in_row) & (sub > lane), sub, SLOTS), axis=0, keepdims=True
    )
    tabled = local(8, table_v, table)
    tabled.wait()
    values_in.wait()
    wide[SLOTS] = jnp.zeros((BLK, BLK), F32)
    for slot in range(SLOTS - 1, -1, -1):
        wide[slot] = values[0, 0, slot].astype(F32) + wide[table[1, slot]]
    for d in range(SPAN * VB):
        for e in range(COLS * VB):
            block = wide[table[0, d * (COLS * VB) + e]].astype(BF16)
            adj[d * BLK:(d + 1) * BLK, e * BLK:(e + 1) * BLK] = block
            adj_t[e * BLK:(e + 1) * BLK, d * BLK:(d + 1) * BLK] = block.T
    for i, rows in enumerate(pieces):
        landed(xg.at[facing, rows], a_recv.at[i])
        send(xg.at[facing, rows], xg.at[facing, rows], a_send, a_recv.at[5], (r, sibling)
        )
    own_x.wait()
    landed(xg.at[sibling], a_recv.at[4])
    for copy in late:
        copy.wait()
    chip = c // 2
    near_lanes = pl.ds(pl.multiple_of(chip * 512, 512), 512)

    def row_block(i):
        return pl.ds(pl.multiple_of(i * 256, 256), 256)

    near = xg[pl.ds(2 * chip, 2)].reshape(512, 256)
    for offset in range(SPAN):
        fwd[offset] = dot(adj[offset * 256:(offset + 1) * 256, near_lanes], near)
    landed(xg.at[behind], a_recv.at[5])
    far_lanes = pl.ds(pl.multiple_of(512 - chip * 512, 512), 512)
    first, second = jnp.where(y < NY // 2, 0, 4), jnp.where(y < NY // 2, 1, 3)

    def mixed_at(offset):
        return fwd[offset] + dot(adj[row_block(offset), far_lanes], xg[pl.ds(2 - 2 * chip, 2)].reshape(512, 256))

    @pl.loop(0, 4)
    def _(i):
        offset = jnp.where(i == 0, first, jnp.where(i == 1, second, jnp.where(i == 2, 4 - first, 4 - second)))
        part[offset] = mixed_at(offset).astype(BF16)
        send(part.at[offset], part_in.at[offset], b_send, b_recv, at_row(offset - HALF))

    mixed = mixed_at(HALF)
    landed(part_in.at[pl.ds(0, 4)], b_recv)
    for offset in (1, 3, 0, 4):
        mixed += part_in[offset].astype(F32)

    high, low = split(mixed)
    pre = dot(high, weight[...]) + dot(low, weight[...]) + bias[...]
    sig = 1.0 / (1.0 + jnp.exp(-pre))
    exact = cot[...].astype(F32) * (sig * (1.0 + pre * (1.0 - sig)))
    grad = exact.astype(BF16)
    g_all[HALF] = grad
    def send_grad(src, dst, distance, arrived):
        send(g_all.at[src], g_all.at[dst], c_send, c_recv.at[arrived], at_row(distance)
        )


    across = (((0,), (0,)), ((), ()))
    w_term = lax.dot_general(high, grad, across, preferred_element_type=F32) + lax.dot_general(
        low, grad, across, preferred_element_type=F32
    )
    w_own[...] = w_term.reshape(8, 32, 256)
    w_out[...] = w_term.reshape(8, 32, 256).astype(BF16)
    bias_k[k] = jnp.sum(exact, axis=0, keepdims=True)
    for step in range(1, 8):
        other = ahead(k, step)
        send(w_out.at[other], w_in.at[k], r_send.at[0], r_recv.at[0], at_k(other)
        )
        send(bias_k.at[k], bias_k.at[k], r_send.at[1], r_recv.at[1], at_k(other)
        )
    send_grad(HALF, 1, 1, 0)
    send_grad(HALF, 3, -1, 1)
    w_in[k] = jnp.zeros((32, 256), BF16)
    out[...] = (pre * sig).astype(BF16)
    landed(w_in.at[pl.ds(0, 7)], r_recv.at[0])
    landed(bias_k.at[pl.ds(0, 7)], r_recv.at[1])
    w_y[y] = (w_own[k] + total_of(w_in)).astype(BF16)
    bias_y[y] = total_of(bias_k)
    for step in range(1, 8):
        other = ahead(y, step)
        send(w_y.at[y], w_y.at[y], r_send.at[2], r_recv.at[2], at_y(other)
        )
        send(bias_y.at[y], bias_y.at[y], r_send.at[3], r_recv.at[3], at_y(other)
        )
    landed(g_all.at[1], c_recv.at[0])
    send_grad(1, 0, 1, 2)
    landed(g_all.at[3], c_recv.at[1])
    send_grad(3, 4, -1, 2)
    close = g_all[pl.ds(1, 3)].reshape(768, 256)
    for j in range(COLS):
        bwd[j] = dot(adj_t[j * 256:(j + 1) * 256, 256:1024], close)
    landed(w_y.at[pl.ds(0, 7)], r_recv.at[2])
    landed(bias_y.at[pl.ds(0, 7)], r_recv.at[3])
    w_z[z] = total_of(w_y).astype(BF16)
    bias_z[z] = total_of(bias_y)
    for step in range(1, 8):
        other = ahead(z, step)
        send(w_z.at[z], w_z.at[z], r_send.at[4], r_recv.at[4], at_z(other)
        )
        send(bias_z.at[z], bias_z.at[z], r_send.at[5], r_recv.at[5], at_z(other)
        )
    landed(g_all.at[pl.ds(0, 2)], c_recv.at[2])

    def finished(j):
        rows = row_block(j)
        return bwd[j] + dot(adj_t[rows, 0:256], g_all[0]) + dot(adj_t[rows, 1024:1280], g_all[4])

    @pl.loop(0, 3)
    def _(i):
        step = jnp.where(i == 0, 2, jnp.where(i == 1, 3, 1))
        other = lax.rem(c + step, COLS)
        term[step] = finished(other).astype(BF16)
        send(term.at[step], term_in.at[c], d_send, d_recv, at_col(step))

    source = finished(c)
    landed(w_z.at[pl.ds(0, 7)], r_recv.at[4])
    landed(bias_z.at[pl.ds(0, 7)], r_recv.at[5])
    normalizer = 1.0 / math.sqrt(256 * ROWS * COLS)
    w_k[k] = (total_of(w_z) * normalizer).astype(BF16)
    for step in range(1, 8):
        other = ahead(k, step)
        send(w_k.at[k], w_k.at[k], r_send.at[6], r_recv.at[6], at_k(other)
        )
    grad_b[...] = total_of(bias_z) * normalizer
    landed(term_in.at[pl.ds(0, 3)], d_recv)
    for step in (1, 2, 3):
        other = lax.rem(c + step, COLS)
        source += term_in[other].astype(F32)
    grad_in[...] = lax.dot_general(
        source.astype(BF16), weight[...], (((1,), (1,)), ((), ())), preferred_element_type=F32
    ).astype(BF16)
    landed(w_k.at[pl.ds(0, 7)], r_recv.at[6])
    grad_w[...] = w_k[...].reshape(256, 256)
    landed(xg.at[pl.ds(0, 3)], a_send)
    landed(part.at[pl.ds(0, 4)], b_send)
    landed(g_all.at[pl.ds(0, 4)], c_send)
    landed(term.at[pl.ds(0, 3)], d_send)
    for i, sent in enumerate((w_out, bias_k, w_y, bias_y, w_z, bias_z, w_k)):
        landed(sent.at[pl.ds(0, 7)], r_send.at[i])


def hand_over(out, grad_in, grad_w, grad_b, out_hbm, grad_in_hbm, grad_w_hbm, grad_b_hbm, wide_w, sems):
    copies = [
        pltpu.make_async_copy(src, dst, sems.at[i])
        for i, (src, dst) in enumerate(
            ((out, out_hbm), (grad_in, grad_in_hbm), (grad_b, grad_b_hbm), (wide_w, grad_w_hbm))
        )
    ]
    for copy in copies[:3]:
        copy.start()
    wide_w[...] = grad_w[...].astype(F32)
    copies[3].start()
    for copy in copies:
        copy.wait()


def shards(
    features, weight, bias, block_values, block_target, block_source, block_count, cotangent
):
    vmem = pl.BlockSpec(memory_space=pltpu.VMEM)
    hbm = pl.BlockSpec(memory_space=pltpu.HBM)
    dma = pltpu.SemaphoreType.DMA
    shapes = [
        jax.ShapeDtypeStruct((256, 256), BF16),
        jax.ShapeDtypeStruct((256, 256), BF16),
        jax.ShapeDtypeStruct((256, 256), BF16),
        jax.ShapeDtypeStruct((1, 256), F32),
    ]
    results = pl.pallas_call(
        layer,
        out_shape=shapes,
        in_specs=[hbm] * 8,
        out_specs=(vmem,) * 4,
        scratch_shapes=[
            pltpu.VMEM((256, 256), BF16),
            pltpu.VMEM((1, 256), F32),
            pltpu.VMEM((256, 256), BF16),
            pltpu.VMEM((1, 1, SLOTS, BLK, BLK), BF16),
            pltpu.SMEM((1, 1, SLOTS), jnp.int32),
            pltpu.SMEM((1, 1, SLOTS), jnp.int32),
            pltpu.SMEM((1, 1), jnp.int32),
            pltpu.VMEM((2, 128), jnp.int32),
            pltpu.SMEM((2, 128), jnp.int32),
            pltpu.VMEM((SLOTS + 1, BLK, BLK), F32),
            pltpu.VMEM((SPAN * 256, COLS * 256), BF16),
            pltpu.VMEM((SPAN, 256, 256), F32),
            pltpu.VMEM((COLS, 256, 256), F32),
            pltpu.VMEM((COLS, 256, 256), BF16),
            pltpu.VMEM((COLS * 256, SPAN * 256), BF16),
            pltpu.VMEM((SPAN, 256, 256), BF16),
            pltpu.VMEM((SPAN, 256, 256), BF16),
            pltpu.VMEM((SPAN, 256, 256), BF16),
            pltpu.VMEM((COLS, 256, 256), BF16),
            pltpu.VMEM((COLS, 256, 256), BF16),
            pltpu.VMEM((8, 32, 256), F32),
            pltpu.VMEM((8, 32, 256), BF16),
            pltpu.VMEM((8, 32, 256), BF16),
            pltpu.VMEM((8, 32, 256), BF16),
            pltpu.VMEM((8, 32, 256), BF16),
            pltpu.VMEM((8, 32, 256), BF16),
            pltpu.VMEM((8, 1, 256), F32),
            pltpu.VMEM((8, 1, 256), F32),
            pltpu.VMEM((8, 1, 256), F32),
            dma((9,)),
            dma,
            dma((6,)),
            dma,
            dma,
            dma,
            dma((3,)),
            dma,
            dma,
            dma((7,)),
            dma((7,)),
        ],
        compiler_params=pltpu.CompilerParams(
            collective_id=0, has_side_effects=True, vmem_limit_bytes=VMEM_BYTES
        ),
        name="layer",
    )(
        features, weight, bias.reshape(1, 256), block_values, block_target, block_source, block_count, cotangent
    )
    output, grad_inputs, grad_weight, grad_bias = pl.pallas_call(
        hand_over,
        out_shape=[*shapes[:2], jax.ShapeDtypeStruct((256, 256), F32), shapes[3]],
        in_specs=[vmem] * 4,
        out_specs=(hbm,) * 4,
        scratch_shapes=[pltpu.VMEM((256, 256), F32), dma((4,))],
        compiler_params=pltpu.CompilerParams(vmem_limit_bytes=1 << 20),
        name="hand_over",
    )(*results)
    return output, grad_inputs, grad_weight, grad_bias.reshape(256)


def solution(mesh):
    return jax.shard_map(
        shards,
        mesh=mesh,
        in_specs=(
            P(("row", "col"), None),
            P(),
            P(),
            P("row", "col", None, None, None),
            P("row", "col", None),
            P("row", "col", None),
            P("row", "col"),
            P(("row", "col"), None),
        ),
        out_specs=(P(("row", "col"), None), P(("row", "col"), None), P(), P()),
        check_vma=False,
    )
```

time: 65.5 us -> 62.3 us (0.951)
  Pallas kernels: 64.1 us -> 60.2 us
  local copies, waits for them, and re-layouts: 0 us -> 0.66 us
    pallas_call x2, Pallas kernels: 64.1 us -> 60.2 us  [the longest x1 59.3 us: shards(): pl.pallas_call(layer, out_shape=shapes, in_specs=[hbm] * 8, out_specs=(vm...]
    unnamed x0 -> x6, local copies, waits for them, and re-layouts: none -> 0.66 us
where the time goes in v3:
time: 62.3 us; the launch traced here: 62.2 us
  Pallas kernels  60.2 us (97%)
  between operations  1.33 us (2%)
  local copies, waits for them, and re-layouts  0.66 us (1%)
    pallas_call x1, Pallas kernels, shards(): pl.pallas_call(layer, out_shape=shapes, in_specs=[hbm] * 8, out_specs=(vm...  59.3 us

profile of v3, /device:TPU:1, one launch (start us, length us, event | category | flops | bytes accessed | tf_op | source)
XLA Modules:
  0.0 62.2 jit_solution(1006897879992624982)
XLA Ops:
  0.6 0.0 copy-start.2
  1.3 0.0 copy-start
  1.3 0.0 copy-start.1
  1.3 0.0 copy-done.2
  1.3 0.7 %copy-done = f32[256]{0:T(256)S(1)} copy-done((f32[256]{0:T(256)S(1)}, f32[256]{0:T(256)}, u32[]{:S(2)}) %copy-start) | copy-done | bytes 1048
  2.0 0.0 copy-done.1
  2.0 59.3 %layer.1 = (bf16[256,256]{1,0:T(8,128)(2,1)S(1)}, bf16[256,256]{1,0:T(8,128)(2,1)S(1)}, bf16[256,256]{1,0:T(8,128)(2,1)S(1)}, f32[1,256]{1,0:T(1,128)S(1)}) custom-call(bf16[256,256]{1,0:T(8,128)(2,1)} %x_hbm.1, bf16[256,256]{1,0:T(8,128)(2,1)} %weight_hbm.1, f32[1,256]{1,0:T(1,128)S(1)} %bitcast.2, bf16[1,1,32,128,128]{4,3,2,1,0:T(8,128)(2,1)} %values_hbm.1, ...), custom_call_target="tpu_custom_call" | custom-call | tf_op jit(solution)/shard_map/layer/pallas_call | solution.py:297
  61.3 0.8 %hand_over.1 = (bf16[256,256]{1,0:T(8,128)(2,1)}, bf16[256,256]{1,0:T(8,128)(2,1)}, f32[256,256]{1,0:T(8,128)}, f32[1,256]{1,0:T(1,128)}) custom-call(bf16[256,256]{1,0:T(8,128)(2,1)S(1)} %get-tuple-element.12.out, bf16[256,256]{1,0:T(8,128)(2,1)S(1)} %get-tuple-element.13.grad_in, bf16[256,256]{1,0:T(8,128)(2,1)S(1)} %get-tuple-element.14.grad_w, ...), custom_call_target="tpu_custom_call" | custom-call | tf_op jit(solution)/shard_map/hand_over/pallas_call | solution.py:351
Async XLA Ops:
  0.6 0.7 %copy-start.2 = (s32[1,1,32]{2,1,0:T(1,128)S(1)}, s32[1,1,32]{2,1,0:T(1,128)}, u32[]{:S(2)}) copy-start(s32[1,1,32]{2,1,0:T(1,128)} %source_hbm.1) | copy-start | bytes 388
  1.3 0.7 %copy-start = (f32[256]{0:T(256)S(1)}, f32[256]{0:T(256)}, u32[]{:S(2)}) copy-start(f32[256]{0:T(256)} %param.10) | copy-start | bytes 3076
  1.3 0.7 %copy-start.1 = (s32[1,1,32]{2,1,0:T(1,128)S(1)}, s32[1,1,32]{2,1,0:T(1,128)}, u32[]{:S(2)}) copy-start(s32[1,1,32]{2,1,0:T(1,128)} %target_hbm.1) | copy-start | bytes 388

commit v4 on v3

--- a/solution.py
+++ b/solution.py
@@ -38,7 +38,7 @@
     weight, bias, cot, values, target, source_of, count, table_v, table, wide, adj, fwd, bwd,
     xg, adj_t, part, part_in, g_all, term, term_in,
     w_own, w_out, w_in, w_z, w_y, w_k, bias_k, bias_z, bias_y,
-    in_sem, a_send, a_recv, b_send, b_recv, c_send, c_recv, d_send, d_recv, r_send, r_recv,
+    in_sem, a_send, a_recv, b_send, b_recv, c_send, c_recv, d_send, d_recv, r_send, r_recv, ready,
 ):
     r = lax.axis_index("row")
     c = lax.axis_index("col")
@@ -91,7 +91,7 @@
     for step in range(1, 8):
         for device in (at_k(ahead(k, step)), at_z(ahead(z, step)), at_y(ahead(y, step))):
             pl.semaphore_signal(barrier, inc=1, device_id=device, device_id_type=MESH)
-    for distance in (1, -1, 2, -2):
+    for distance in (-1, -2):
         pl.semaphore_signal(barrier, inc=1, device_id=at_row(distance), device_id_type=MESH)
     scalars = [
         local(0, target_hbm, target),
@@ -101,7 +101,9 @@
     own_x = local(3, x_hbm, xg.at[c])
     values_in = local(4, values_hbm, values)
     late = [local(5, weight_hbm, weight), local(6, bias_hbm, bias), local(7, cot_hbm, cot)]
-    pl.semaphore_wait(barrier, 4 + 3 * 7)
+    pl.semaphore_wait(barrier, 2 + 3 * 7)
+    for distance in (1, 2):
+        pl.semaphore_signal(ready, inc=1, device_id=at_row(distance), device_id_type=MESH)
     sibling = c + 1 - 2 * lax.rem(c, 2)
     facing = lax.rem(c + 2, COLS)
     behind = lax.rem(sibling + 2, COLS)
@@ -137,36 +139,34 @@
             block = wide[table[0, d * (COLS * VB) + e]].astype(BF16)
             adj[d * BLK:(d + 1) * BLK, e * BLK:(e + 1) * BLK] = block
             adj_t[e * BLK:(e + 1) * BLK, d * BLK:(d + 1) * BLK] = block.T
+    own_x.wait()
+    landed(xg.at[sibling], a_recv.at[4])
+    chip = c // 2
+    near = xg[pl.ds(2 * chip, 2)].reshape(512, 256)
+    near_lanes = pl.ds(pl.multiple_of(chip * 512, 512), 512)
+    for offset in range(SPAN):
+        fwd[offset] = dot(adj[offset * 256:(offset + 1) * 256, near_lanes], near)
     for i, rows in enumerate(pieces):
         landed(xg.at[facing, rows], a_recv.at[i])
-        send(xg.at[facing, rows], xg.at[facing, rows], a_send, a_recv.at[5], (r, sibling)
-        )
-    own_x.wait()
-    landed(xg.at[sibling], a_recv.at[4])
+        send(xg.at[facing, rows], xg.at[facing, rows], a_send, a_recv.at[5], (r, sibling))
+
+    def row_block(i):
+        return pl.ds(pl.multiple_of(i * 256, 256), 256)
+
+    for offset in range(SPAN):
+        fwd[offset] += dot(adj[offset * 256:(offset + 1) * 256, row_block(facing)], xg[facing])
     for copy in late:
         copy.wait()
-    chip = c // 2
-    near_lanes = pl.ds(pl.multiple_of(chip * 512, 512), 512)
-
-    def row_block(i):
-        return pl.ds(pl.multiple_of(i * 256, 256), 256)
-
-    near = xg[pl.ds(2 * chip, 2)].reshape(512, 256)
-    for offset in range(SPAN):
-        fwd[offset] = dot(adj[offset * 256:(offset + 1) * 256, near_lanes], near)
     landed(xg.at[behind], a_recv.at[5])
-    far_lanes = pl.ds(pl.multiple_of(512 - chip * 512, 512), 512)
     first, second = jnp.where(y < NY // 2, 0, 4), jnp.where(y < NY // 2, 1, 3)
 
     def mixed_at(offset):
-        return fwd[offset] + dot(adj[row_block(offset), far_lanes], xg[pl.ds(2 - 2 * chip, 2)].reshape(512, 256))
-
-    @pl.loop(0, 4)
-    def _(i):
-        offset = jnp.where(i == 0, first, jnp.where(i == 1, second, jnp.where(i == 2, 4 - first, 4 - second)))
+        return fwd[offset] + dot(adj[row_block(offset), row_block(behind)], xg[behind])
+
+    pl.semaphore_wait(ready, 2)
+    for offset in (first, second, 4 - first, 4 - second):
         part[offset] = mixed_at(offset).astype(BF16)
         send(part.at[offset], part_in.at[offset], b_send, b_recv, at_row(offset - HALF))
-
     mixed = mixed_at(HALF)
     landed(part_in.at[pl.ds(0, 4)], b_recv)
     for offset in (1, 3, 0, 4):
@@ -233,14 +233,14 @@
         rows = row_block(j)
         return bwd[j] + dot(adj_t[rows, 0:256], g_all[0]) + dot(adj_t[rows, 1024:1280], g_all[4])
 
-    @pl.loop(0, 3)
-    def _(i):
-        step = jnp.where(i == 0, 2, jnp.where(i == 1, 3, 1))
-        other = lax.rem(c + step, COLS)
-        term[step] = finished(other).astype(BF16)
-        send(term.at[step], term_in.at[c], d_send, d_recv, at_col(step))
-
-    source = finished(c)
+    for i, other in enumerate((behind, sibling)):
+        term[i] = finished(other).astype(BF16)
+        send(term.at[i], term_in.at[i], d_send, d_recv.at[i], (r, sibling))
+    bwd[facing] = finished(facing)
+    bwd[c] = finished(c)
+    landed(term_in.at[0], d_recv.at[0])
+    term[2] = (bwd[facing] + term_in[0].astype(F32)).astype(BF16)
+    send(term.at[2], term_in.at[2], d_send, d_recv.at[2], (r, facing))
     landed(w_z.at[pl.ds(0, 7)], r_recv.at[4])
     landed(bias_z.at[pl.ds(0, 7)], r_recv.at[5])
     normalizer = 1.0 / math.sqrt(256 * ROWS * COLS)
@@ -250,10 +250,9 @@
         send(w_k.at[k], w_k.at[k], r_send.at[6], r_recv.at[6], at_k(other)
         )
     grad_b[...] = total_of(bias_z) * normalizer
-    landed(term_in.at[pl.ds(0, 3)], d_recv)
-    for step in (1, 2, 3):
-        other = lax.rem(c + step, COLS)
-        source += term_in[other].astype(F32)
+    landed(term_in.at[1], d_recv.at[1])
+    landed(term_in.at[2], d_recv.at[2])
+    source = bwd[c] + term_in[1].astype(F32) + term_in[2].astype(F32)
     grad_in[...] = lax.dot_general(
         source.astype(BF16), weight[...], (((1,), (1,)), ((), ())), preferred_element_type=F32
     ).astype(BF16)
@@ -337,9 +336,10 @@
             dma,
             dma((3,)),
             dma,
-            dma,
+            dma((3,)),
             dma((7,)),
             dma((7,)),
+            pltpu.SemaphoreType.REGULAR,
         ],
         compiler_params=pltpu.CompilerParams(
             collective_id=0, has_side_effects=True, vmem_limit_bytes=VMEM_BYTES

time: 62.3 us -> 59.4 us (0.953)
  Pallas kernels: 60.2 us -> 57.3 us
    pallas_call x1, Pallas kernels: 59.3 us -> 56.5 us  [shards(): pl.pallas_call(layer, out_shape=shapes, in_specs=[hbm] * 8, out_specs=(vm...]
where the time goes in v4:
time: 59.4 us; the launch traced here: 59.3 us
  Pallas kernels  57.3 us (96%)
  between operations  1.33 us (2%)
  local copies, waits for them, and re-layouts  0.66 us (1%)
    pallas_call x1, Pallas kernels, shards(): pl.pallas_call(layer, out_shape=shapes, in_specs=[hbm] * 8, out_specs=(vm...  56.5 us

profile of v4, /device:TPU:1, one launch (start us, length us, event | category | flops | bytes accessed | tf_op | source)
XLA Modules:
  0.0 59.3 jit_solution(4711018734545729224)
XLA Ops:
  0.6 0.0 copy-start.2
  1.3 0.0 copy-start
  1.3 0.0 copy-start.1
  1.3 0.0 copy-done.2
  1.3 0.7 %copy-done = f32[256]{0:T(256)S(1)} copy-done((f32[256]{0:T(256)S(1)}, f32[256]{0:T(256)}, u32[]{:S(2)}) %copy-start) | copy-done | bytes 1048
  2.0 0.0 copy-done.1
  2.0 56.5 %layer.1 = (bf16[256,256]{1,0:T(8,128)(2,1)S(1)}, bf16[256,256]{1,0:T(8,128)(2,1)S(1)}, bf16[256,256]{1,0:T(8,128)(2,1)S(1)}, f32[1,256]{1,0:T(1,128)S(1)}) custom-call(bf16[256,256]{1,0:T(8,128)(2,1)} %x_hbm.1, bf16[256,256]{1,0:T(8,128)(2,1)} %weight_hbm.1, f32[1,256]{1,0:T(1,128)S(1)} %bitcast.2, bf16[1,1,32,128,128]{4,3,2,1,0:T(8,128)(2,1)} %values_hbm.1, ...), custom_call_target="tpu_custom_call" | custom-call | tf_op jit(solution)/shard_map/layer/pallas_call | solution.py:296
  58.5 0.8 %hand_over.1 = (bf16[256,256]{1,0:T(8,128)(2,1)}, bf16[256,256]{1,0:T(8,128)(2,1)}, f32[256,256]{1,0:T(8,128)}, f32[1,256]{1,0:T(1,128)}) custom-call(bf16[256,256]{1,0:T(8,128)(2,1)S(1)} %get-tuple-element.12.out, bf16[256,256]{1,0:T(8,128)(2,1)S(1)} %get-tuple-element.13.grad_in, bf16[256,256]{1,0:T(8,128)(2,1)S(1)} %get-tuple-element.14.grad_w, ...), custom_call_target="tpu_custom_call" | custom-call | tf_op jit(solution)/shard_map/hand_over/pallas_call | solution.py:351
Async XLA Ops:
  0.6 0.7 %copy-start.2 = (s32[1,1,32]{2,1,0:T(1,128)S(1)}, s32[1,1,32]{2,1,0:T(1,128)}, u32[]{:S(2)}) copy-start(s32[1,1,32]{2,1,0:T(1,128)} %source_hbm.1) | copy-start | bytes 388
  1.3 0.7 %copy-start = (f32[256]{0:T(256)S(1)}, f32[256]{0:T(256)}, u32[]{:S(2)}) copy-start(f32[256]{0:T(256)} %param.10) | copy-start | bytes 3076
  1.3 0.7 %copy-start.1 = (s32[1,1,32]{2,1,0:T(1,128)S(1)}, s32[1,1,32]{2,1,0:T(1,128)}, u32[]{:S(2)}) copy-start(s32[1,1,32]{2,1,0:T(1,128)} %target_hbm.1) | copy-start | bytes 388

commit v5 on v4

--- a/solution.py
+++ b/solution.py
@@ -87,12 +87,39 @@
         copy.start()
         return copy
 
+    def turn(place):
+        return jnp.where(place < NY // 2, place, 3 * NY // 2 - 1 - place)
+
+    def rank(row):
+        return (4 * (row // (2 * NY)) + turn(lax.rem(row, NY))) * ROWS + row
+
+    def signal(sem, device):
+        pl.semaphore_signal(sem, inc=1, device_id=device, device_id_type=MESH)
+
     barrier = pltpu.get_barrier_semaphore()
-    for step in range(1, 8):
-        for device in (at_k(ahead(k, step)), at_z(ahead(z, step)), at_y(ahead(y, step))):
-            pl.semaphore_signal(barrier, inc=1, device_id=device, device_id_type=MESH)
-    for distance in (-1, -2):
-        pl.semaphore_signal(barrier, inc=1, device_id=at_row(distance), device_id_type=MESH)
+    my_turn = turn(y)
+    for step in range(1, COLS):
+        signal(barrier, at_col(step))
+    leads = []
+    for distance in (1, -1, 2, -2):
+        lead = rank(r) < rank(lax.rem(r + distance + ROWS, ROWS))
+        leads.append(lead)
+        pl.when(lead)(lambda distance=distance: signal(barrier, at_row(distance)))
+
+    @pl.when(xh == 0)
+    def _():
+        for j in range(COLS):
+            signal(barrier, at_k(COLS + j))
+
+    @pl.loop(my_turn + 1, NY)
+    def _(other):
+        signal(barrier, at_y(turn(other)))
+
+    @pl.loop(z + 1, NZ)
+    def _(other):
+        signal(barrier, at_z(other))
+
+    followed = sum(jnp.where(lead, 0, 1) for lead in leads)
     scalars = [
         local(0, target_hbm, target),
         local(1, source_hbm, source_of),
@@ -101,9 +128,7 @@
     own_x = local(3, x_hbm, xg.at[c])
     values_in = local(4, values_hbm, values)
     late = [local(5, weight_hbm, weight), local(6, bias_hbm, bias), local(7, cot_hbm, cot)]
-    pl.semaphore_wait(barrier, 2 + 3 * 7)
-    for distance in (1, 2):
-        pl.semaphore_signal(ready, inc=1, device_id=at_row(distance), device_id_type=MESH)
+    pl.semaphore_wait(barrier, COLS - 1 + COLS * xh + my_turn + z + followed)
     sibling = c + 1 - 2 * lax.rem(c, 2)
     facing = lax.rem(c + 2, COLS)
     behind = lax.rem(sibling + 2, COLS)
@@ -112,6 +137,22 @@
         send(x_hbm.at[rows], xg.at[c, rows], a_send, a_recv.at[i], (r, facing)
         )
     send(x_hbm, xg.at[c], a_send, a_recv.at[4], (r, sibling))
+    for distance, lead in zip((1, -1, 2, -2), leads):
+        pl.when(jnp.logical_not(lead))(lambda distance=distance: signal(ready.at[0], at_row(distance)))
+
+    @pl.when(xh == 1)
+    def _():
+        for j in range(COLS):
+            signal(ready.at[1], at_k(j))
+
+    @pl.loop(0, my_turn)
+    def _(other):
+        signal(ready.at[1], at_y(turn(other)))
+
+    @pl.loop(0, z)
+    def _(other):
+        signal(ready.at[1], at_z(other))
+
     for copy in scalars:
         copy.wait()
     lane = lax.broadcasted_iota(jnp.int32, (SLOTS, 128), 1)
@@ -163,7 +204,7 @@
     def mixed_at(offset):
         return fwd[offset] + dot(adj[row_block(offset), row_block(behind)], xg[behind])
 
-    pl.semaphore_wait(ready, 2)
+    pl.when(followed < 4)(lambda: pl.semaphore_wait(ready.at[0], 4 - followed))
     for offset in (first, second, 4 - first, 4 - second):
         part[offset] = mixed_at(offset).astype(BF16)
         send(part.at[offset], part_in.at[offset], b_send, b_recv, at_row(offset - HALF))
@@ -183,6 +224,8 @@
         )
 
 
+    answers = COLS * (1 - xh) + (NY - 1 - my_turn) + (NZ - 1 - z)
+    pl.when(answers > 0)(lambda: pl.semaphore_wait(ready.at[1], answers))
     across = (((0,), (0,)), ((), ()))
     w_term = lax.dot_general(high, grad, across, preferred_element_type=F32) + lax.dot_general(
         low, grad, across, preferred_element_type=F32
@@ -339,7 +382,7 @@
             dma((3,)),
             dma((7,)),
             dma((7,)),
-            pltpu.SemaphoreType.REGULAR,
+            pltpu.SemaphoreType.REGULAR((2,)),
         ],
         compiler_params=pltpu.CompilerParams(
             collective_id=0, has_side_effects=True, vmem_limit_bytes=VMEM_BYTES

time: 59.4 us -> 58.7 us (0.988)
  Pallas kernels: 57.3 us -> 56.6 us
    pallas_call x1, Pallas kernels: 56.5 us -> 55.7 us  [shards(): pl.pallas_call(layer, out_shape=shapes, in_specs=[hbm] * 8, out_specs=(vm...]
where the time goes in v5:
time: 58.7 us; the launch traced here: 58.5 us
  Pallas kernels  56.6 us (96%)
  between operations  1.33 us (2%)
  local copies, waits for them, and re-layouts  0.66 us (1%)
    pallas_call x1, Pallas kernels, shards(): pl.pallas_call(layer, out_shape=shapes, in_specs=[hbm] * 8, out_specs=(vm...  55.7 us

profile of v5, /device:TPU:1, one launch (start us, length us, event | category | flops | bytes accessed | tf_op | source)
XLA Modules:
  0.0 58.5 jit_solution(8387213940232897122)
XLA Ops:
  0.6 0.0 copy-start.2
  1.3 0.0 copy-start
  1.3 0.0 copy-start.1
  1.3 0.0 copy-done.2
  1.3 0.7 %copy-done = f32[256]{0:T(256)S(1)} copy-done((f32[256]{0:T(256)S(1)}, f32[256]{0:T(256)}, u32[]{:S(2)}) %copy-start) | copy-done | bytes 1048
  2.0 0.0 copy-done.1
  2.0 55.7 %layer.1 = (bf16[256,256]{1,0:T(8,128)(2,1)S(1)}, bf16[256,256]{1,0:T(8,128)(2,1)S(1)}, bf16[256,256]{1,0:T(8,128)(2,1)S(1)}, f32[1,256]{1,0:T(1,128)S(1)}) custom-call(bf16[256,256]{1,0:T(8,128)(2,1)} %x_hbm.1, bf16[256,256]{1,0:T(8,128)(2,1)} %weight_hbm.1, f32[1,256]{1,0:T(1,128)S(1)} %bitcast.2, bf16[1,1,32,128,128]{4,3,2,1,0:T(8,128)(2,1)} %values_hbm.1, ...), custom_call_target="tpu_custom_call" | custom-call | tf_op jit(solution)/shard_map/layer/pallas_call | solution.py:339
  57.7 0.8 %hand_over.1 = (bf16[256,256]{1,0:T(8,128)(2,1)}, bf16[256,256]{1,0:T(8,128)(2,1)}, f32[256,256]{1,0:T(8,128)}, f32[1,256]{1,0:T(1,128)}) custom-call(bf16[256,256]{1,0:T(8,128)(2,1)S(1)} %get-tuple-element.12.out, bf16[256,256]{1,0:T(8,128)(2,1)S(1)} %get-tuple-element.13.grad_in, bf16[256,256]{1,0:T(8,128)(2,1)S(1)} %get-tuple-element.14.grad_w, ...), custom_call_target="tpu_custom_call" | custom-call | tf_op jit(solution)/shard_map/hand_over/pallas_call | solution.py:394
Async XLA Ops:
  0.6 0.7 %copy-start.2 = (s32[1,1,32]{2,1,0:T(1,128)S(1)}, s32[1,1,32]{2,1,0:T(1,128)}, u32[]{:S(2)}) copy-start(s32[1,1,32]{2,1,0:T(1,128)} %source_hbm.1) | copy-start | bytes 388
  1.3 0.7 %copy-start = (f32[256]{0:T(256)S(1)}, f32[256]{0:T(256)}, u32[]{:S(2)}) copy-start(f32[256]{0:T(256)} %param.10) | copy-start | bytes 3076
  1.3 0.7 %copy-start.1 = (s32[1,1,32]{2,1,0:T(1,128)S(1)}, s32[1,1,32]{2,1,0:T(1,128)}, u32[]{:S(2)}) copy-start(s32[1,1,32]{2,1,0:T(1,128)} %target_hbm.1) | copy-start | bytes 388

commit v6 on v5

--- a/solution.py
+++ b/solution.py
@@ -101,7 +101,7 @@
     for step in range(1, COLS):
         signal(barrier, at_col(step))
     leads = []
-    for distance in (1, -1, 2, -2):
+    for distance in (1, -1):
         lead = rank(r) < rank(lax.rem(r + distance + ROWS, ROWS))
         leads.append(lead)
         pl.when(lead)(lambda distance=distance: signal(barrier, at_row(distance)))
@@ -134,10 +134,10 @@
     behind = lax.rem(sibling + 2, COLS)
     pieces = [pl.ds(64 * i, 64) for i in range(4)]
     for i, rows in enumerate(pieces):
-        send(x_hbm.at[rows], xg.at[c, rows], a_send, a_recv.at[i], (r, facing)
-        )
+        send(x_hbm.at[rows], xg.at[c, rows], a_send, a_recv.at[i], (r, facing))
+    send(x_hbm.at[pieces[3]], xg.at[c, pieces[3]], a_send, a_recv.at[5], (r, behind))
     send(x_hbm, xg.at[c], a_send, a_recv.at[4], (r, sibling))
-    for distance, lead in zip((1, -1, 2, -2), leads):
+    for distance, lead in zip((1, -1), leads):
         pl.when(jnp.logical_not(lead))(lambda distance=distance: signal(ready.at[0], at_row(distance)))
 
     @pl.when(xh == 1)
@@ -189,7 +189,8 @@
         fwd[offset] = dot(adj[offset * 256:(offset + 1) * 256, near_lanes], near)
     for i, rows in enumerate(pieces):
         landed(xg.at[facing, rows], a_recv.at[i])
-        send(xg.at[facing, rows], xg.at[facing, rows], a_send, a_recv.at[5], (r, sibling))
+        if i < 3:
+            send(xg.at[facing, rows], xg.at[facing, rows], a_send, a_recv.at[5], (r, sibling))
 
     def row_block(i):
         return pl.ds(pl.multiple_of(i * 256, 256), 256)
@@ -199,20 +200,24 @@
     for copy in late:
         copy.wait()
     landed(xg.at[behind], a_recv.at[5])
-    first, second = jnp.where(y < NY // 2, 0, 4), jnp.where(y < NY // 2, 1, 3)
+    first = jnp.where(y < NY // 2, 0, 4)
 
     def mixed_at(offset):
         return fwd[offset] + dot(adj[row_block(offset), row_block(behind)], xg[behind])
 
-    pl.when(followed < 4)(lambda: pl.semaphore_wait(ready.at[0], 4 - followed))
-    for offset in (first, second, 4 - first, 4 - second):
+    pl.when(followed < 2)(lambda: pl.semaphore_wait(ready.at[0], 2 - followed))
+    for offset in (first, 4 - first):
         part[offset] = mixed_at(offset).astype(BF16)
-        send(part.at[offset], part_in.at[offset], b_send, b_recv, at_row(offset - HALF))
-    mixed = mixed_at(HALF)
-    landed(part_in.at[pl.ds(0, 4)], b_recv)
-    for offset in (1, 3, 0, 4):
-        mixed += part_in[offset].astype(F32)
-
+        send(part.at[offset], part_in.at[offset], b_send, b_recv.at[offset // 4], at_row(offset // 2 - 1))
+    for offset in (1, 3, HALF):
+        fwd[offset] = mixed_at(offset)
+    for offset in (first, 4 - first):
+        landed(part_in.at[offset], b_recv.at[offset // 4])
+        onward = offset // 2 + 1
+        part[onward] = (fwd[onward] + part_in[offset].astype(F32)).astype(BF16)
+        send(part.at[onward], part_in.at[onward], b_send, b_recv.at[2], at_row(offset // 2 - 1))
+    landed(part_in.at[pl.ds(0, 2)], b_recv.at[2])
+    mixed = fwd[HALF] + part_in[1].astype(F32) + part_in[3].astype(F32)
     high, low = split(mixed)
     pre = dot(high, weight[...]) + dot(low, weight[...]) + bias[...]
     sig = 1.0 / (1.0 + jnp.exp(-pre))
@@ -220,8 +225,7 @@
     grad = exact.astype(BF16)
     g_all[HALF] = grad
     def send_grad(src, dst, distance, arrived):
-        send(g_all.at[src], g_all.at[dst], c_send, c_recv.at[arrived], at_row(distance)
-        )
+        send(g_all.at[src], g_all.at[dst], c_send, c_recv.at[arrived], at_row(distance))
 
 
     answers = COLS * (1 - xh) + (NY - 1 - my_turn) + (NZ - 1 - z)
@@ -235,10 +239,8 @@
     bias_k[k] = jnp.sum(exact, axis=0, keepdims=True)
     for step in range(1, 8):
         other = ahead(k, step)
-        send(w_out.at[other], w_in.at[k], r_send.at[0], r_recv.at[0], at_k(other)
-        )
-        send(bias_k.at[k], bias_k.at[k], r_send.at[1], r_recv.at[1], at_k(other)
-        )
+        send(w_out.at[other], w_in.at[k], r_send.at[0], r_recv.at[0], at_k(other))
+        send(bias_k.at[k], bias_k.at[k], r_send.at[1], r_recv.at[1], at_k(other))
     send_grad(HALF, 1, 1, 0)
     send_grad(HALF, 3, -1, 1)
     w_in[k] = jnp.zeros((32, 256), BF16)
@@ -249,10 +251,8 @@
     bias_y[y] = total_of(bias_k)
     for step in range(1, 8):
         other = ahead(y, step)
-        send(w_y.at[y], w_y.at[y], r_send.at[2], r_recv.at[2], at_y(other)
-        )
-        send(bias_y.at[y], bias_y.at[y], r_send.at[3], r_recv.at[3], at_y(other)
-        )
+        send(w_y.at[y], w_y.at[y], r_send.at[2], r_recv.at[2], at_y(other))
+        send(bias_y.at[y], bias_y.at[y], r_send.at[3], r_recv.at[3], at_y(other))
     landed(g_all.at[1], c_recv.at[0])
     send_grad(1, 0, 1, 2)
     landed(g_all.at[3], c_recv.at[1])
@@ -266,10 +266,8 @@
     bias_z[z] = total_of(bias_y)
     for step in range(1, 8):
         other = ahead(z, step)
-        send(w_z.at[z], w_z.at[z], r_send.at[4], r_recv.at[4], at_z(other)
-        )
-        send(bias_z.at[z], bias_z.at[z], r_send.at[5], r_recv.at[5], at_z(other)
-        )
+        send(w_z.at[z], w_z.at[z], r_send.at[4], r_recv.at[4], at_z(other))
+        send(bias_z.at[z], bias_z.at[z], r_send.at[5], r_recv.at[5], at_z(other))
     landed(g_all.at[pl.ds(0, 2)], c_recv.at[2])
 
     def finished(j):
@@ -290,8 +288,7 @@
     w_k[k] = (total_of(w_z) * normalizer).astype(BF16)
     for step in range(1, 8):
         other = ahead(k, step)
-        send(w_k.at[k], w_k.at[k], r_send.at[6], r_recv.at[6], at_k(other)
-        )
+        send(w_k.at[k], w_k.at[k], r_send.at[6], r_recv.at[6], at_k(other))
     grad_b[...] = total_of(bias_z) * normalizer
     landed(term_in.at[1], d_recv.at[1])
     landed(term_in.at[2], d_recv.at[2])
@@ -313,8 +310,7 @@
     copies = [
         pltpu.make_async_copy(src, dst, sems.at[i])
         for i, (src, dst) in enumerate(
-            ((out, out_hbm), (grad_in, grad_in_hbm), (grad_b, grad_b_hbm), (wide_w, grad_w_hbm))
-        )
+            ((out, out_hbm), (grad_in, grad_in_hbm), (grad_b, grad_b_hbm), (wide_w, grad_w_hbm)))
     ]
     for copy in copies[:3]:
         copy.start()
@@ -375,7 +371,7 @@
             dma,
             dma((6,)),
             dma,
-            dma,
+            dma((3,)),
             dma,
             dma((3,)),
             dma,

time: 58.7 us -> 57.2 us (0.974)
  Pallas kernels: 56.6 us -> 55.1 us
    pallas_call x1, Pallas kernels: 55.7 us -> 54.2 us  [shards(): pl.pallas_call(layer, out_shape=shapes, in_specs=[hbm] * 8, out_specs=(vm...]
where the time goes in v6:
time: 57.2 us; the launch traced here: 57.1 us
  Pallas kernels  55.1 us (96%)
  between operations  1.33 us (2%)
  local copies, waits for them, and re-layouts  0.66 us (1%)
    pallas_call x1, Pallas kernels, shards(): pl.pallas_call(layer, out_shape=shapes, in_specs=[hbm] * 8, out_specs=(vm...  54.2 us

profile of v6, /device:TPU:1, one launch (start us, length us, event | category | flops | bytes accessed | tf_op | source)
XLA Modules:
  0.0 57.1 jit_solution(8248776184716727192)
XLA Ops:
  0.6 0.0 copy-start.2
  1.3 0.0 copy-start
  1.3 0.0 copy-start.1
  1.3 0.0 copy-done.2
  1.3 0.7 %copy-done = f32[256]{0:T(256)S(1)} copy-done((f32[256]{0:T(256)S(1)}, f32[256]{0:T(256)}, u32[]{:S(2)}) %copy-start) | copy-done | bytes 1048
  2.0 0.0 copy-done.1
  2.0 54.2 %layer.1 = (bf16[256,256]{1,0:T(8,128)(2,1)S(1)}, bf16[256,256]{1,0:T(8,128)(2,1)S(1)}, bf16[256,256]{1,0:T(8,128)(2,1)S(1)}, f32[1,256]{1,0:T(1,128)S(1)}) custom-call(bf16[256,256]{1,0:T(8,128)(2,1)} %x_hbm.1, bf16[256,256]{1,0:T(8,128)(2,1)} %weight_hbm.1, f32[1,256]{1,0:T(1,128)S(1)} %bitcast.2, bf16[1,1,32,128,128]{4,3,2,1,0:T(8,128)(2,1)} %values_hbm.1, ...), custom_call_target="tpu_custom_call" | custom-call | tf_op jit(solution)/shard_map/layer/pallas_call | solution.py:335
  56.2 0.8 %hand_over.1 = (bf16[256,256]{1,0:T(8,128)(2,1)}, bf16[256,256]{1,0:T(8,128)(2,1)}, f32[256,256]{1,0:T(8,128)}, f32[1,256]{1,0:T(1,128)}) custom-call(bf16[256,256]{1,0:T(8,128)(2,1)S(1)} %get-tuple-element.12.out, bf16[256,256]{1,0:T(8,128)(2,1)S(1)} %get-tuple-element.13.grad_in, bf16[256,256]{1,0:T(8,128)(2,1)S(1)} %get-tuple-element.14.grad_w, ...), custom_call_target="tpu_custom_call" | custom-call | tf_op jit(solution)/shard_map/hand_over/pallas_call | solution.py:390
Async XLA Ops:
  0.6 0.7 %copy-start.2 = (s32[1,1,32]{2,1,0:T(1,128)S(1)}, s32[1,1,32]{2,1,0:T(1,128)}, u32[]{:S(2)}) copy-start(s32[1,1,32]{2,1,0:T(1,128)} %source_hbm.1) | copy-start | bytes 388
  1.3 0.7 %copy-start = (f32[256]{0:T(256)S(1)}, f32[256]{0:T(256)}, u32[]{:S(2)}) copy-start(f32[256]{0:T(256)} %param.10) | copy-start | bytes 3076
  1.3 0.7 %copy-start.1 = (s32[1,1,32]{2,1,0:T(1,128)S(1)}, s32[1,1,32]{2,1,0:T(1,128)}, u32[]{:S(2)}) copy-start(s32[1,1,32]{2,1,0:T(1,128)} %target_hbm.1) | copy-start | bytes 388

commit v7 on v6

--- a/solution.py
+++ b/solution.py
@@ -16,6 +16,7 @@
 NY = 8
 NZ = 8
 SLOTS = 32
+FAR_FIRST = (4, 3, 5, 2, 6, 1, 7)
 VMEM_BYTES = 54810 << 10
 CELLS = SPAN * VB * COLS * VB
 MESH = pl.DeviceIdType.MESH
@@ -228,6 +229,8 @@
         send(g_all.at[src], g_all.at[dst], c_send, c_recv.at[arrived], at_row(distance))
 
 
+    send_grad(HALF, 1, 1, 0)
+    send_grad(HALF, 3, -1, 1)
     answers = COLS * (1 - xh) + (NY - 1 - my_turn) + (NZ - 1 - z)
     pl.when(answers > 0)(lambda: pl.semaphore_wait(ready.at[1], answers))
     across = (((0,), (0,)), ((), ()))
@@ -237,19 +240,17 @@
     w_own[...] = w_term.reshape(8, 32, 256)
     w_out[...] = w_term.reshape(8, 32, 256).astype(BF16)
     bias_k[k] = jnp.sum(exact, axis=0, keepdims=True)
-    for step in range(1, 8):
+    for step in FAR_FIRST:
         other = ahead(k, step)
         send(w_out.at[other], w_in.at[k], r_send.at[0], r_recv.at[0], at_k(other))
         send(bias_k.at[k], bias_k.at[k], r_send.at[1], r_recv.at[1], at_k(other))
-    send_grad(HALF, 1, 1, 0)
-    send_grad(HALF, 3, -1, 1)
     w_in[k] = jnp.zeros((32, 256), BF16)
     out[...] = (pre * sig).astype(BF16)
     landed(w_in.at[pl.ds(0, 7)], r_recv.at[0])
     landed(bias_k.at[pl.ds(0, 7)], r_recv.at[1])
     w_y[y] = (w_own[k] + total_of(w_in)).astype(BF16)
     bias_y[y] = total_of(bias_k)
-    for step in range(1, 8):
+    for step in FAR_FIRST:
         other = ahead(y, step)
         send(w_y.at[y], w_y.at[y], r_send.at[2], r_recv.at[2], at_y(other))
         send(bias_y.at[y], bias_y.at[y], r_send.at[3], r_recv.at[3], at_y(other))
@@ -264,7 +265,7 @@
     landed(bias_y.at[pl.ds(0, 7)], r_recv.at[3])
     w_z[z] = total_of(w_y).astype(BF16)
     bias_z[z] = total_of(bias_y)
-    for step in range(1, 8):
+    for step in FAR_FIRST:
         other = ahead(z, step)
         send(w_z.at[z], w_z.at[z], r_send.at[4], r_recv.at[4], at_z(other))
         send(bias_z.at[z], bias_z.at[z], r_send.at[5], r_recv.at[5], at_z(other))
@@ -286,7 +287,7 @@
     landed(bias_z.at[pl.ds(0, 7)], r_recv.at[5])
     normalizer = 1.0 / math.sqrt(256 * ROWS * COLS)
     w_k[k] = (total_of(w_z) * normalizer).astype(BF16)
-    for step in range(1, 8):
+    for step in FAR_FIRST:
         other = ahead(k, step)
         send(w_k.at[k], w_k.at[k], r_send.at[6], r_recv.at[6], at_k(other))
     grad_b[...] = total_of(bias_z) * normalizer

time: 57.2 us -> 56.4 us (0.986)
  Pallas kernels: 55.1 us -> 54.2 us
    pallas_call x1, Pallas kernels: 54.2 us -> 53.4 us  [shards(): pl.pallas_call(layer, out_shape=shapes, in_specs=[hbm] * 8, out_specs=(vm...]
where the time goes in v7:
time: 56.4 us; the launch traced here: 56.2 us
  Pallas kernels  54.2 us (96%)
  between operations  1.33 us (2%)
  local copies, waits for them, and re-layouts  0.66 us (1%)
    pallas_call x1, Pallas kernels, shards(): pl.pallas_call(layer, out_shape=shapes, in_specs=[hbm] * 8, out_specs=(vm...  53.4 us

profile of v7, /device:TPU:1, one launch (start us, length us, event | category | flops | bytes accessed | tf_op | source)
XLA Modules:
  0.0 56.2 jit_solution(690960065136162650)
XLA Ops:
  0.6 0.0 copy-start.2
  1.3 0.0 copy-start
  1.3 0.0 copy-start.1
  1.3 0.0 copy-done.2
  1.3 0.7 %copy-done = f32[256]{0:T(256)S(1)} copy-done((f32[256]{0:T(256)S(1)}, f32[256]{0:T(256)}, u32[]{:S(2)}) %copy-start) | copy-done | bytes 1048
  2.0 0.0 copy-done.1
  2.0 53.4 %layer.1 = (bf16[256,256]{1,0:T(8,128)(2,1)S(1)}, bf16[256,256]{1,0:T(8,128)(2,1)S(1)}, bf16[256,256]{1,0:T(8,128)(2,1)S(1)}, f32[1,256]{1,0:T(1,128)S(1)}) custom-call(bf16[256,256]{1,0:T(8,128)(2,1)} %x_hbm.1, bf16[256,256]{1,0:T(8,128)(2,1)} %weight_hbm.1, f32[1,256]{1,0:T(1,128)S(1)} %bitcast.2, bf16[1,1,32,128,128]{4,3,2,1,0:T(8,128)(2,1)} %values_hbm.1, ...), custom_call_target="tpu_custom_call" | custom-call | tf_op jit(solution)/shard_map/layer/pallas_call | solution.py:336
  55.4 0.8 %hand_over.1 = (bf16[256,256]{1,0:T(8,128)(2,1)}, bf16[256,256]{1,0:T(8,128)(2,1)}, f32[256,256]{1,0:T(8,128)}, f32[1,256]{1,0:T(1,128)}) custom-call(bf16[256,256]{1,0:T(8,128)(2,1)S(1)} %get-tuple-element.12.out, bf16[256,256]{1,0:T(8,128)(2,1)S(1)} %get-tuple-element.13.grad_in, bf16[256,256]{1,0:T(8,128)(2,1)S(1)} %get-tuple-element.14.grad_w, ...), custom_call_target="tpu_custom_call" | custom-call | tf_op jit(solution)/shard_map/hand_over/pallas_call | solution.py:391
Async XLA Ops:
  0.6 0.7 %copy-start.2 = (s32[1,1,32]{2,1,0:T(1,128)S(1)}, s32[1,1,32]{2,1,0:T(1,128)}, u32[]{:S(2)}) copy-start(s32[1,1,32]{2,1,0:T(1,128)} %source_hbm.1) | copy-start | bytes 388
  1.3 0.7 %copy-start = (f32[256]{0:T(256)S(1)}, f32[256]{0:T(256)}, u32[]{:S(2)}) copy-start(f32[256]{0:T(256)} %param.10) | copy-start | bytes 3076
  1.3 0.7 %copy-start.1 = (s32[1,1,32]{2,1,0:T(1,128)S(1)}, s32[1,1,32]{2,1,0:T(1,128)}, u32[]{:S(2)}) copy-start(s32[1,1,32]{2,1,0:T(1,128)} %target_hbm.1) | copy-start | bytes 388

commit v8 on v7

--- a/solution.py
+++ b/solution.py
@@ -207,17 +207,21 @@
         return fwd[offset] + dot(adj[row_block(offset), row_block(behind)], xg[behind])
 
     pl.when(followed < 2)(lambda: pl.semaphore_wait(ready.at[0], 2 - followed))
+    halves = (pl.ds(0, 128), pl.ds(128, 128))
     for offset in (first, 4 - first):
         part[offset] = mixed_at(offset).astype(BF16)
-        send(part.at[offset], part_in.at[offset], b_send, b_recv.at[offset // 4], at_row(offset // 2 - 1))
+        for i, rows in enumerate(halves):
+            send(
+                part.at[offset, rows], part_in.at[offset, rows], b_send, b_recv.at[offset // 2 + i], at_row(offset // 2 - 1))
     for offset in (1, 3, HALF):
         fwd[offset] = mixed_at(offset)
-    for offset in (first, 4 - first):
-        landed(part_in.at[offset], b_recv.at[offset // 4])
-        onward = offset // 2 + 1
-        part[onward] = (fwd[onward] + part_in[offset].astype(F32)).astype(BF16)
-        send(part.at[onward], part_in.at[onward], b_send, b_recv.at[2], at_row(offset // 2 - 1))
-    landed(part_in.at[pl.ds(0, 2)], b_recv.at[2])
+    for i, rows in enumerate(halves):
+        for offset in (first, 4 - first):
+            landed(part_in.at[offset, rows], b_recv.at[offset // 2 + i])
+            onward = offset // 2 + 1
+            part[onward, rows] = (fwd[onward, rows] + part_in[offset, rows].astype(F32)).astype(BF16)
+            send(part.at[onward, rows], part_in.at[onward, rows], b_send, b_recv.at[4], at_row(offset // 2 - 1))
+    landed(part_in.at[pl.ds(0, 2)], b_recv.at[4])
     mixed = fwd[HALF] + part_in[1].astype(F32) + part_in[3].astype(F32)
     high, low = split(mixed)
     pre = dot(high, weight[...]) + dot(low, weight[...]) + bias[...]
@@ -372,7 +376,7 @@
             dma,
             dma((6,)),
             dma,
-            dma((3,)),
+            dma((5,)),
             dma,
             dma((3,)),
             dma,

time: 56.4 us -> 57 us (1.011)
  Pallas kernels: 54.2 us -> 54.8 us
    pallas_call x1, Pallas kernels: 53.4 us -> 54 us  [shards(): pl.pallas_call(layer, out_shape=shapes, in_specs=[hbm] * 8, out_specs=(vm...]
where the time goes in v8:
time: 57 us; the launch traced here: 56.8 us
  Pallas kernels  54.8 us (96%)
  between operations  1.33 us (2%)
  local copies, waits for them, and re-layouts  0.66 us (1%)
    pallas_call x1, Pallas kernels, shards(): pl.pallas_call(layer, out_shape=shapes, in_specs=[hbm] * 8, out_specs=(vm...  54 us

profile of v8, /device:TPU:1, one launch (start us, length us, event | category | flops | bytes accessed | tf_op | source)
XLA Modules:
  0.0 56.8 jit_solution(4169133639499441400)
XLA Ops:
  0.6 0.0 copy-start.2
  1.3 0.0 copy-start
  1.3 0.0 copy-start.1
  1.3 0.0 copy-done.2
  1.3 0.7 %copy-done = f32[256]{0:T(256)S(1)} copy-done((f32[256]{0:T(256)S(1)}, f32[256]{0:T(256)}, u32[]{:S(2)}) %copy-start) | copy-done | bytes 1048
  2.0 0.0 copy-done.1
  2.0 54.0 %layer.1 = (bf16[256,256]{1,0:T(8,128)(2,1)S(1)}, bf16[256,256]{1,0:T(8,128)(2,1)S(1)}, bf16[256,256]{1,0:T(8,128)(2,1)S(1)}, f32[1,256]{1,0:T(1,128)S(1)}) custom-call(bf16[256,256]{1,0:T(8,128)(2,1)} %x_hbm.1, bf16[256,256]{1,0:T(8,128)(2,1)} %weight_hbm.1, f32[1,256]{1,0:T(1,128)S(1)} %bitcast.2, bf16[1,1,32,128,128]{4,3,2,1,0:T(8,128)(2,1)} %values_hbm.1, ...), custom_call_target="tpu_custom_call" | custom-call | tf_op jit(solution)/shard_map/layer/pallas_call | solution.py:340
  56.0 0.8 %hand_over.1 = (bf16[256,256]{1,0:T(8,128)(2,1)}, bf16[256,256]{1,0:T(8,128)(2,1)}, f32[256,256]{1,0:T(8,128)}, f32[1,256]{1,0:T(1,128)}) custom-call(bf16[256,256]{1,0:T(8,128)(2,1)S(1)} %get-tuple-element.12.out, bf16[256,256]{1,0:T(8,128)(2,1)S(1)} %get-tuple-element.13.grad_in, bf16[256,256]{1,0:T(8,128)(2,1)S(1)} %get-tuple-element.14.grad_w, ...), custom_call_target="tpu_custom_call" | custom-call | tf_op jit(solution)/shard_map/hand_over/pallas_call | solution.py:395
Async XLA Ops:
  0.6 0.7 %copy-start.2 = (s32[1,1,32]{2,1,0:T(1,128)S(1)}, s32[1,1,32]{2,1,0:T(1,128)}, u32[]{:S(2)}) copy-start(s32[1,1,32]{2,1,0:T(1,128)} %source_hbm.1) | copy-start | bytes 388
  1.3 0.7 %copy-start = (f32[256]{0:T(256)S(1)}, f32[256]{0:T(256)}, u32[]{:S(2)}) copy-start(f32[256]{0:T(256)} %param.10) | copy-start | bytes 3076
  1.3 0.7 %copy-start.1 = (s32[1,1,32]{2,1,0:T(1,128)S(1)}, s32[1,1,32]{2,1,0:T(1,128)}, u32[]{:S(2)}) copy-start(s32[1,1,32]{2,1,0:T(1,128)} %target_hbm.1) | copy-start | bytes 388
